TPU v7x, 32 devices: a whole 2x2x4 slice. The times are simulated.
32 devices in a mesh: groups: 2 (over y), blk: 4 (over z), team: 2 (over x), head: 2 (over core).
Axes of the slice: x: 2, y: 2, z: 4, core: 2. Of those that a mesh axis runs over, the one named last changes fastest.
Arguments:
- queries: bfloat16 [768, 2560], P(('groups', 'blk', 'team'), 'head'), parts along dimension 0, may hold values from -8 to 8
- key_rows: bfloat16 [768, 2560], P(('groups', 'blk', 'team'), 'head'), parts along dimension 0, may hold values from -8 to 8
- value_rows: bfloat16 [768, 2560], P(('groups', 'blk', 'team'), 'head'), parts along dimension 0, may hold values from -6 to 6
Outputs:
- attended: bfloat16 [768, 2560], P(('groups', 'blk', 'team'), 'head'), parts along dimension 0
There are 2 independent parts, one for each index of `groups`. A program takes and returns all parts, laid end to end along the dimension named above; each array names one. Nothing has to cross between parts.
All inputs are finite; a program needn't handle non-finite values.
Results may differ from a plain program's by a relative error of at most 0.009.
Values may be sent and summed in bfloat16 or wider, within the bound.
No kernel may reach another device: no remote copies, remote signals or barrier semaphores. Data moves between devices by JAX's collectives and lax.ppermute only.
A program may use at most 64 MiB of HBM per device.

v0:
```python
from functools import partial
import math

import jax
import jax.numpy as jnp
from jax import lax
from jax.sharding import PartitionSpec as P

HD = 128
T_DEV = 48


def attend_block(running, key_block, value_block, query_rows, score_scale):
    row_top, row_total, weighted = running
    scores = (
        jnp.einsum("qhd,khd->qhk", query_rows, key_block, preferred_element_type=jnp.float32)
        * score_scale
    )
    new_top = jnp.maximum(row_top, jnp.max(scores, axis=2))
    shrink = jnp.exp(row_top - new_top)
    weights = jnp.exp(scores - new_top[:, :, None])
    row_total = row_total * shrink + jnp.sum(weights, axis=2)
    weighted = weighted * shrink[:, :, None] + jnp.einsum(
        "qhk,khd->qhd",
        weights.astype(jnp.bfloat16),
        value_block,
        preferred_element_type=jnp.float32,
    )
    return (new_top, row_total, weighted)


def fold_piece(running, shard_piece, first_row, query_rows, score_scale):
    key_piece, value_piece = shard_piece
    piece_rows = key_piece.shape[0]
    block_rows = T_DEV
    local_heads = query_rows.shape[1]
    key_blocks = key_piece.reshape(piece_rows // block_rows, block_rows, local_heads, HD)
    value_blocks = value_piece.reshape(piece_rows // block_rows, block_rows, local_heads, HD)

    def one_block(current, block_pair):
        return (attend_block(current, block_pair[0], block_pair[1], query_rows, score_scale), None)

    running, unused = lax.scan(one_block, running, (key_blocks, value_blocks))
    return running


def local(queries, key_rows, value_rows):
    own_rows = queries.shape[0]
    local_heads = queries.shape[1] // HD
    score_scale = 1.0 / math.sqrt(HD)
    team_queries = lax.all_gather(queries, "team", axis=0, tiled=True)
    team_count = team_queries.shape[0]
    query_heads = team_queries.reshape(team_count, local_heads, HD)
    folder = partial(fold_piece, query_rows=query_heads, score_scale=score_scale)
    row_top, row_total, weighted = folder(
        (
            jnp.full((team_count, local_heads), -1e30, jnp.float32),
            jnp.zeros((team_count, local_heads), jnp.float32),
            jnp.zeros((team_count, local_heads, HD), jnp.float32),
        ),
        (
            lax.all_gather(key_rows, "blk", axis=0, tiled=True),
            lax.all_gather(value_rows, "blk", axis=0, tiled=True),
        ),
        jnp.int32(0),
    )
    swapped, member_tops, totals = (
        lax.all_to_all(
            weighted.reshape(team_count, local_heads * HD),
            "team",
            split_axis=0,
            concat_axis=0,
            tiled=True,
        ),
        lax.all_to_all(row_top, "team", split_axis=0, concat_axis=0, tiled=True),
        lax.all_to_all(row_total, "team", split_axis=0, concat_axis=0, tiled=True),
    )
    members = lax.axis_size("team")
    member_tops = member_tops.reshape(members, own_rows, local_heads)
    common_top = jnp.max(member_tops, axis=0)
    factor = jnp.exp(member_tops - common_top[None])
    row_sum = jnp.sum(factor * totals.reshape(members, own_rows, local_heads), axis=0)
    summed = jnp.sum(
        factor[:, :, :, None] * swapped.reshape(members, own_rows, local_heads, HD), axis=0
    )
    mixed_rows = summed / row_sum[:, :, None]
    return mixed_rows.reshape(own_rows, local_heads * HD).astype(jnp.bfloat16)


def solution(mesh):
    in_specs = (
        P(("groups", "blk", "team"), "head"),
        P(("groups", "blk", "team"), "head"),
        P(("groups", "blk", "team"), "head"),
    )
    out_specs = P(("groups", "blk", "team"), "head")
    return jax.shard_map(local, mesh=mesh, in_specs=in_specs, out_specs=out_specs, check_vma=False)
```

profile of v0, /device:TPU:0, one launch (start us, length us, event | category | flops | bytes accessed | tf_op | source)
XLA Modules:
  0.0 70.4 jit_solution(14824911914724854757)
XLA Ops:
  0.0 17.3 %all_gather.9 = bf16[192,1280]{1,0:T(8,128)(2,1)S(1)} all-gather(bf16[48,1280]{1,0:T(8,128)(2,1)} %param.6), channel_id=1, replica_groups=mesh['groups'=2,'blk'=4,'team'=2,'head'=2] {'blk'}, dimensions={0}, use_global_device_ids=true | all-gather | bytes 614400 | tf_op jit(solution)/shard_map/all_gather | solution.py:62
  17.3 0.3 reshape.38
  17.6 0.0 copy-start
  17.6 0.1 copy.20
  17.8 0.8 %copy-done = bf16[48,1280]{1,0:T(8,128)(2,1)S(1)} copy-done((bf16[48,1280]{1,0:T(8,128)(2,1)S(1)}, bf16[48,1280]{1,0:T(8,128)(2,1)}, u32[]{:S(2)}) %copy-start) | copy-done | bytes 122904
  18.5 16.0 %all_gather.11 = bf16[192,1280]{1,0:T(8,128)(2,1)S(1)} all-gather(bf16[48,1280]{1,0:T(8,128)(2,1)S(1)} %copy-done), channel_id=1, replica_groups=mesh['groups'=2,'blk'=4,'team'=2,'head'=2] {'blk'}, dimensions={0}, use_global_device_ids=true | all-gather | bytes 614400 | tf_op jit(solution)/shard_map/all_gather | solution.py:63
  34.5 0.3 reshape.40
  34.8 0.1 copy.22
  35.0 0.8 %copy-done.1 = bf16[48,1280]{1,0:T(8,128)(2,1)S(1)} copy-done((bf16[48,1280]{1,0:T(8,128)(2,1)S(1)}, bf16[48,1280]{1,0:T(8,128)(2,1)}, u32[]{:S(2)}) %copy-start.1) | copy-done | bytes 122904
  35.7 5.5 %all_gather.10 = bf16[96,1280]{1,0:T(8,128)(2,1)S(1)} all-gather(bf16[48,1280]{1,0:T(8,128)(2,1)S(1)} %copy-done.1), channel_id=1, replica_groups=mesh['groups'=2,'blk'=4,'team'=2,'head'=2] {'team'}, dimensions={0}, use_global_device_ids=true | all-gather | bytes 368640 | tf_op jit(solution)/shard_map/all_gather | solution.py:51
  41.3 0.2 copy.19
  41.5 0.2 copy.21
  41.7 3.1 %while.15 = (s32[]{:T(128)}, f32[96,10]{0,1:T(8,128)S(1)}, f32[96,10]{0,1:T(8,128)S(1)}, f32[96,10,128]{2,0,1:T(8,128)S(1)}, bf16[4,48,10,128]{3,1,2,0:T(8,128)(...) while((s32[]{:T(128)}, f32[96,10]{0,1:T(8,128)S(1)}, ...), condition=%wide.region_3.4_spmd.clone, body=%wide.region_0.3_spmd.clone.sunk | while | flops 24242884 | bytes 2159217 | solution.py:43
  41.7 0.3 fusion.26
  42.0 0.1 fusion.27
  42.1 0.3 fusion.29
  42.5 0.3 fusion.26
  42.8 0.1 fusion.27
  42.9 0.3 fusion.29
  43.3 0.3 fusion.26
  43.6 0.1 fusion.27
  43.7 0.3 fusion.29
  44.0 0.3 fusion.26
  44.3 0.1 fusion.27
  44.4 0.3 fusion.29
  44.8 0.1 all_to_all.18
  44.9 0.7 reshape.41
  45.6 3.2 %all-to-all-start = ((f32[2,1,480]{2,1,0:T(1,128)}), f32[2,1,480]{2,1,0:T(1,128)S(1)}, u32[]{:S(2)}, u32[]{:S(2)}) async-start(f32[2,1,480]{2,1,0:T(1,128)} %reshape.41), calls=%async_computation | async-start | bytes 8192 | tf_op jit(solution)/shard_map/all_to_all | solution.py:75
  48.8 0.1 all_to_all.22
  48.9 0.7 reshape.43
  49.6 3.0 %all-to-all-done = f32[2,1,480]{2,1,0:T(1,128)S(1)} async-done(((f32[2,1,480]{2,1,0:T(1,128)}), f32[2,1,480]{2,1,0:T(1,128)S(1)}, u32[]{:S(2)}, u32[]{:S(2)}) %all-to-all-start) | async-done | bytes 3872 | tf_op jit(solution)/shard_map/all_to_all | solution.py:75
  52.6 3.2 %all-to-all-start.2 = ((f32[2,1,480]{2,1,0:T(1,128)}), f32[2,1,480]{2,1,0:T(1,128)S(1)}, u32[]{:S(2)}, u32[]{:S(2)}) async-start(f32[2,1,480]{2,1,0:T(1,128)} %reshape.43), calls=%async_computation.2 | async-start | bytes 8192 | tf_op jit(solution)/shard_map/all_to_all | solution.py:76
  55.8 0.3 copy.25
  56.1 0.9 %all_to_all.20 = f32[2,48,1280]{2,1,0:T(8,128)} reshape(f32[96,10,128]{2,1,0:T(8,128)S(1)} %copy.25) | data formatting | bytes 983040 | tf_op jit(solution)/shard_map/all_to_all | solution.py:68
  56.9 0.5 broadcast.38
  57.5 0.7 reduce.2
  58.1 0.1 reshape.42
  58.2 1.3 %all-to-all-done.2 = f32[2,1,480]{2,1,0:T(1,128)S(1)} async-done(((f32[2,1,480]{2,1,0:T(1,128)}), f32[2,1,480]{2,1,0:T(1,128)S(1)}, u32[]{:S(2)}, u32[]{:S(2)}) %all-to-all-start.2) | async-done | bytes 3872 | tf_op jit(solution)/shard_map/all_to_all | solution.py:76
  59.6 3.5 %all-to-all-start.1 = ((f32[2,48,1280]{2,1,0:T(8,128)}), f32[2,48,1280]{2,1,0:T(8,128)S(1)}, u32[]{:S(2)}, u32[]{:S(2)}) async-start(f32[2,48,1280]{2,1,0:T(8,128)} %all_to_all.20), calls=%async_computation.1 | async-start | bytes 983040 | tf_op jit(solution)/shard_map/all_to_all | solution.py:68
  63.1 0.7 reduce.3
  63.7 0.1 reshape.44
  63.8 0.1 copy.24
  63.9 0.3 mul.31
  64.2 0.1 mul.32
  64.3 0.1 copy.28
  64.4 5.1 %all-to-all-done.1 = f32[2,48,1280]{2,1,0:T(8,128)S(1)} async-done(((f32[2,48,1280]{2,1,0:T(8,128)}), f32[2,48,1280]{2,1,0:T(8,128)S(1)}, u32[]{:S(2)}, u32[]{:S(2)}) %all-to-all-start.1) | async-done | bytes 491552 | tf_op jit(solution)/shard_map/all_to_all | solution.py:68
  69.5 0.2 div.11
  69.6 0.7 %fusion.13 = bf16[48,1280]{1,0:T(8,128)(2,1)} fusion(f32[48,1280]{1,0:T(8,128)S(1)} %multiply_reduce_fusion, f32[6,8,10,128]{3,2,1,0:T(8,128)S(1)} %bitcast.44), kind=kLoop, calls=%fused_computation.21 | loop fusion | flops 122880 | bytes 614400 | tf_op jit(solution)/shard_map/convert_element_type | solution.py:87
  (21 shorter events, 0.2 us)
Async XLA Ops:
  17.6 0.9 %copy-start = (bf16[48,1280]{1,0:T(8,128)(2,1)S(1)}, bf16[48,1280]{1,0:T(8,128)(2,1)}, u32[]{:S(2)}) copy-start(bf16[48,1280]{1,0:T(8,128)(2,1)} %param.7) | copy-start | bytes 368644
  34.8 0.9 %copy-start.1 = (bf16[48,1280]{1,0:T(8,128)(2,1)S(1)}, bf16[48,1280]{1,0:T(8,128)(2,1)}, u32[]{:S(2)}) copy-start(bf16[48,1280]{1,0:T(8,128)(2,1)} %param.5) | copy-start | bytes 368644
  45.6 7.0 %all-to-all-start = ((f32[2,1,480]{2,1,0:T(1,128)}), f32[2,1,480]{2,1,0:T(1,128)S(1)}, u32[]{:S(2)}, u32[]{:S(2)}) async-start(f32[2,1,480]{2,1,0:T(1,128)} %reshape.41), calls=%async_computation | async-start | bytes 8192 | tf_op jit(solution)/shard_map/all_to_all | solution.py:75
  52.6 7.0 %all-to-all-start.2 = ((f32[2,1,480]{2,1,0:T(1,128)}), f32[2,1,480]{2,1,0:T(1,128)S(1)}, u32[]{:S(2)}, u32[]{:S(2)}) async-start(f32[2,1,480]{2,1,0:T(1,128)} %reshape.43), calls=%async_computation.2 | async-start | bytes 8192 | tf_op jit(solution)/shard_map/all_to_all | solution.py:76
  59.6 9.9 %all-to-all-start.1 = ((f32[2,48,1280]{2,1,0:T(8,128)}), f32[2,48,1280]{2,1,0:T(8,128)S(1)}, u32[]{:S(2)}, u32[]{:S(2)}) async-start(f32[2,48,1280]{2,1,0:T(8,128)} %all_to_all.20), calls=%async_computation.1 | async-start | bytes 983040 | tf_op jit(solution)/shard_map/all_to_all | solution.py:68
where the time goes:
time: 70.8 us; the launch traced here: 70.4 us
  blocking collectives  38.9 us (55%)
  starting transfers between devices  9.91 us (14%)
  waiting for transfers between devices  9.42 us (13%)
  local copies, waits for them, and re-layouts  6.86 us (10%)
  matrix products  2.52 us (4%)
  other arithmetic  2.46 us (3%)
    all_gather x1, blocking collectives, local(): lax.all_gather(key_rows, 'blk', axis=0, tiled=True)  17.3 us
    all_gather x1, blocking collectives, local(): lax.all_gather(value_rows, 'blk', axis=0, tiled=True)  16 us
    all_gather x1, blocking collectives, local(): team_queries = lax.all_gather(queries, 'team', axis=0, tiled=True)  5.54 us
    all_to_all x1, waiting for transfers between devices, local(): lax.all_to_all(weighted.reshape(team_count, local_heads * HD), 'team', sp...  5.06 us
    unnamed x11, local copies, waits for them, and re-layouts  3.5 us
    all_to_all x1, starting transfers between devices, local(): lax.all_to_all(weighted.reshape(team_count, local_heads * HD), 'team', sp...  3.48 us
    all_to_all x1, starting transfers between devices, local(): lax.all_to_all(row_top, 'team', split_axis=0, concat_axis=0, tiled=True)  3.22 us
    all_to_all x1, starting transfers between devices, local(): lax.all_to_all(row_total, 'team', split_axis=0, concat_axis=0, tiled=True)  3.21 us
  transfers between devices with their start and end apart: 3, of which 3 were waited for; matrix products, arithmetic and copies ran while one was open for 5% of the time, Pallas kernels for 0%

commit v1 on v0

--- a/solution.py
+++ b/solution.py
@@ -4,7 +4,10 @@
 import jax
 import jax.numpy as jnp
 from jax import lax
+from jax.experimental import pallas as pl
+from jax.experimental.pallas import tpu as pltpu
 from jax.sharding import PartitionSpec as P
+
 
 HD = 128
 T_DEV = 48
@@ -29,7 +32,7 @@
     return (new_top, row_total, weighted)
 
 
-def fold_piece(running, shard_piece, first_row, query_rows, score_scale):
+def fold_piece(running, shard_piece, query_rows, score_scale):
     key_piece, value_piece = shard_piece
     piece_rows = key_piece.shape[0]
     block_rows = T_DEV
@@ -40,11 +43,11 @@
     def one_block(current, block_pair):
         return (attend_block(current, block_pair[0], block_pair[1], query_rows, score_scale), None)
 
-    running, unused = lax.scan(one_block, running, (key_blocks, value_blocks))
+    running, _ = lax.scan(one_block, running, (key_blocks, value_blocks))
     return running
 
 
-def local(queries, key_rows, value_rows):
+def gathered(queries, key_rows, value_rows):
     own_rows = queries.shape[0]
     local_heads = queries.shape[1] // HD
     score_scale = 1.0 / math.sqrt(HD)
@@ -62,7 +65,6 @@
             lax.all_gather(key_rows, "blk", axis=0, tiled=True),
             lax.all_gather(value_rows, "blk", axis=0, tiled=True),
         ),
-        jnp.int32(0),
     )
     swapped, member_tops, totals = (
         lax.all_to_all(
@@ -87,11 +89,207 @@
     return mixed_rows.reshape(own_rows, local_heads * HD).astype(jnp.bfloat16)
 
 
+TOPS, PARTS = 3, 5
+GAP = 128 // 8
+
+
+def vmem_spec():
+    return pl.BlockSpec(memory_space=pltpu.VMEM)
+
+
+def hbm_array(array):
+    return pltpu.with_memory_space_constraint(array, pltpu.HBM)
+
+
+def params():
+    return pltpu.CompilerParams(vmem_limit_bytes=16 * 2**20)
+
+
+def pack_kernel(width, pieces, *refs):
+    n_outs = len(pieces)
+    sems = refs[-1]
+    args, outs = refs[: -1 - n_outs], refs[-1 - n_outs : -1]
+    rows = args[0].shape[0]
+    own = lax.rem(lax.axis_index("team"), 2)
+    halves = [pl.ds(pl.multiple_of(h * width, HD), width) for h in (own, 1 - own)]
+    copies = []
+    for parts, out in zip(pieces, outs):
+        for i, (arg, half) in enumerate(parts):
+            source = args[arg].at[:, halves[half]]
+            target = out.at[pl.ds(i * rows, rows)]
+            copies.append(pltpu.make_async_copy(source, target, sems.at[len(copies)]))
+            copies[-1].start()
+    for copy in copies:
+        copy.wait()
+
+
+def pack(pieces, *arrays):
+    rows, width = arrays[0].shape[0], arrays[0].shape[1] // 2
+    return pl.pallas_call(
+        partial(pack_kernel, width, pieces),
+        out_shape=[
+            jax.ShapeDtypeStruct((len(parts) * rows, width), arrays[0].dtype) for parts in pieces
+        ],
+        in_specs=[pl.BlockSpec(memory_space=pltpu.HBM)] * len(arrays),
+        out_specs=[vmem_spec()] * len(pieces),
+        scratch_shapes=[pltpu.SemaphoreType.DMA((sum(map(len, pieces)),))],
+        compiler_params=params(),
+        name="pack",
+    )(*map(hbm_array, arrays))
+
+
+def attend_kernel(rows, n_keys, *refs):
+    kv_refs, rest = refs[:n_keys], refs[n_keys:]
+    n_queries = len(rest) // 2
+    q_refs, o_refs = rest[:n_queries], rest[n_queries:]
+    width = q_refs[0].shape[1]
+    scale = 1.0 / math.sqrt(HD)
+    lane = lax.broadcasted_iota(jnp.int32, (n_queries * rows, HD), 1)
+    slot, part = lax.rem(lane, GAP), lax.div(lane, GAP)
+    stats = jnp.zeros((n_queries * rows, HD), jnp.float32)
+    for h in range(width // HD):
+        columns = slice(h * HD, (h + 1) * HD)
+        q = jnp.concatenate([ref[ref.shape[0] - rows :, columns] for ref in q_refs], axis=0)
+        k = jnp.concatenate([ref[:rows, columns] for ref in kv_refs], axis=0)
+        v = jnp.concatenate([ref[rows : 2 * rows, columns] for ref in kv_refs], axis=0)
+        scores = (
+            lax.dot_general(q, k, (((1,), (1,)), ((), ())), preferred_element_type=jnp.float32)
+            * scale
+        )
+        top = jnp.max(scores, axis=1, keepdims=True)
+        weights = jnp.exp(scores - top)
+        total = jnp.sum(weights, axis=1, keepdims=True)
+        mixed = jnp.dot(weights.astype(jnp.bfloat16), v, preferred_element_type=jnp.float32)
+        mixed = mixed.astype(jnp.bfloat16)
+        stats = jnp.where(slot == h, jnp.where(part < TOPS, top, total), stats)
+        for i, ref in enumerate(o_refs):
+            ref[:, columns] = mixed[i * rows : (i + 1) * rows]
+    first = stats.astype(jnp.bfloat16).astype(jnp.float32)
+    left = stats - first
+    second = left.astype(jnp.bfloat16).astype(jnp.float32)
+    is_second = (part == 1) | (part == TOPS + 1)
+    stats = jnp.where(is_second, second, jnp.where(part == 2, left - second, first))
+    stats = stats.astype(jnp.bfloat16)
+    for i, ref in enumerate(o_refs):
+        ref[:, width:] = stats[i * rows : (i + 1) * rows]
+
+
+def merge_kernel(*refs):
+    pieces, out_ref = refs[:-1], refs[-1]
+    width = pieces[0].shape[1] - HD
+    tops, totals = [], []
+    for ref in pieces:
+        stats = ref[:, width:].astype(jnp.float32)
+        shifted = [stats] + [pltpu.roll(stats, HD - i * GAP, 1) for i in range(1, PARTS)]
+        tops.append(shifted[0] + shifted[1] + shifted[2])
+        totals.append(shifted[3] + shifted[4])
+    common = tops[0]
+    for top in tops[1:]:
+        common = jnp.maximum(common, top)
+    factors = [jnp.exp(top - common) for top in tops]
+    row_sum = sum(f * t for f, t in zip(factors, totals))
+    factors = [f / row_sum for f in factors]
+    for h in range(width // HD):
+        columns = slice(h * HD, (h + 1) * HD)
+        mixed = sum(
+            f[:, h : h + 1] * ref[:, columns].astype(jnp.float32) for f, ref in zip(factors, pieces)
+        )
+        out_ref[:, columns] = mixed.astype(out_ref.dtype)
+
+
+def finish_kernel(other_ref, own_ref, answer_ref, out_ref, own_half, sems):
+    width = other_ref.shape[1]
+    half = lax.rem(lax.axis_index("team"), 2)
+    copies = [
+        pltpu.make_async_copy(
+            source, out_ref.at[:, pl.ds(pl.multiple_of(which * width, HD), width)], sems.at[i]
+        )
+        for i, (source, which) in enumerate(((other_ref, 1 - half), (own_half, half)))
+    ]
+    copies[0].start()
+    merge_kernel(own_ref, answer_ref, own_half)
+    copies[1].start()
+    for copy in copies:
+        copy.wait()
+
+
+def paired(queries, key_rows, value_rows):
+    rows = queries.shape[0]
+    width = queries.shape[1] // 2
+    planes, members = lax.axis_size("blk"), lax.axis_size("team")
+
+    def shape(n_rows, columns):
+        return jax.ShapeDtypeStruct((n_rows, columns), queries.dtype)
+
+    def send(array, plane_bits, member_bits):
+        pairs = [
+            (z * members + m, (z ^ plane_bits) * members + (m ^ member_bits))
+            for z in range(planes)
+            for m in range(members)
+        ]
+        return lax.ppermute(array, ("blk", "team"), pairs)
+
+    kv_own, kv_other, kvq_other, q_own, q_other = pack(
+        (
+            ((0, 0), (1, 0)),
+            ((0, 1), (1, 1)),
+            ((0, 1), (1, 1), (2, 1)),
+            ((2, 0),),
+            ((2, 1),),
+        ),
+        key_rows,
+        value_rows,
+        queries,
+    )
+
+    near = send(kvq_other, 0, 1)
+    keys = [kv_own, near]
+    for plane_bits, member_bits in key_sends(planes, members):
+        array = kv_other if member_bits % 2 else kv_own
+        keys.append(send(array, plane_bits, member_bits))
+    asked = [q_own, near, send(q_own, 1, 0), send(q_other, 1, 1)]
+    own, *answers = pl.pallas_call(
+        partial(attend_kernel, rows, len(keys)),
+        out_shape=[shape(rows, width + HD)] * len(asked),
+        in_specs=[vmem_spec()] * (len(keys) + len(asked)),
+        out_specs=[vmem_spec()] * len(asked),
+        compiler_params=params(),
+        name="attend",
+    )(*keys, *asked)
+    back_near = send(answers[0], 0, 1)
+    back_ask = send(answers[1], 1, 0)
+    back_cross = send(answers[2], 1, 1)
+    early = pl.pallas_call(
+        merge_kernel,
+        out_shape=shape(rows, width),
+        in_specs=[vmem_spec()] * 2,
+        out_specs=vmem_spec(),
+        compiler_params=params(),
+        name="merge",
+    )(back_near, back_cross)
+    return pl.pallas_call(
+        finish_kernel,
+        out_shape=shape(rows, 2 * width),
+        in_specs=[vmem_spec()] * 3,
+        out_specs=pl.BlockSpec(memory_space=pl.ANY),
+        scratch_shapes=[pltpu.VMEM((rows, width), queries.dtype), pltpu.SemaphoreType.DMA((2,))],
+        compiler_params=params(),
+        name="finish",
+    )(early, own, back_ask)
+
+
+def key_sends(planes, members):
+    return [(p, m) for p in range(0, planes, 2) for m in range(members) if p or m > 1]
+
+
 def solution(mesh):
-    in_specs = (
-        P(("groups", "blk", "team"), "head"),
-        P(("groups", "blk", "team"), "head"),
-        P(("groups", "blk", "team"), "head"),
-    )
-    out_specs = P(("groups", "blk", "team"), "head")
-    return jax.shard_map(local, mesh=mesh, in_specs=in_specs, out_specs=out_specs, check_vma=False)
+    spec = P(("groups", "blk", "team"), "head")
+    planes, members = mesh.shape["blk"], mesh.shape["team"]
+    in_quads = all(n > 1 and n & (n - 1) == 0 for n in (planes, members))
+
+    def local(queries, key_rows, value_rows):
+        heads = queries.shape[1] // HD
+        plan = paired if in_quads and heads % 2 == 0 and heads // 2 <= GAP else gathered
+        return plan(queries, key_rows, value_rows)
+
+    return jax.shard_map(local, mesh=mesh, in_specs=(spec,) * 3, out_specs=spec, check_vma=False)

time: 70.8 us -> 26.7 us (0.38)
  blocking collectives: 38.9 us -> 0 us
  local copies, waits for them, and re-layouts: 6.86 us -> 0 us
  Pallas kernels: 0 us -> 3.11 us
  matrix products: 2.52 us -> 0 us
  starting transfers between devices: 9.91 us -> 12.4 us
  other arithmetic: 2.46 us -> 0 us
  waiting for transfers between devices: 9.42 us -> 11 us
    all_gather x3 -> x0, blocking collectives: 38.9 us -> none  [the longest x1 17.3 us: local(): lax.all_gather(key_rows, 'blk', axis=0, tiled=True)]
    ppermute x0 -> x8, starting transfers between devices: none -> 12.4 us  [send(): return lax.ppermute(array, ('blk', 'team'), pairs)]
    ppermute x0 -> x8, waiting for transfers between devices: none -> 11 us  [send(): return lax.ppermute(array, ('blk', 'team'), pairs)]
    all_to_all x3 -> x0, starting transfers between devices: 9.91 us -> none  [the longest x1 3.48 us: local(): lax.all_to_all(weighted.reshape(team_count, local_heads * HD), 'team', sp...]
    all_to_all x3 -> x0, waiting for transfers between devices: 9.42 us -> none  [the longest x1 5.06 us: local(): lax.all_to_all(weighted.reshape(team_count, local_heads * HD), 'team', sp...]
    unnamed x11 -> x0, local copies, waits for them, and re-layouts: 3.5 us -> none
    pallas_call x0 -> x4, Pallas kernels: none -> 3.11 us  [the longest x1 1.14 us: pack(): pl.pallas_call(partial(pack_kernel, width, pieces), out_shape=[jax.ShapeD...]
    dot_general x8 -> x0, matrix products: 2.52 us -> none  [the longest x4 1.37 us: attend_block(): jnp.einsum('qhk,khd->qhd', weights.astype(jnp.bfloat16), value_block, pre...]
  transfers between devices with their start and end apart: 3 -> 8, of which waited for: 3 -> 6; matrix products, arithmetic and copies ran while one was open for 5% -> 0% of each run, Pallas kernels for 0% -> 1%
where the time goes in v1:
time: 26.7 us; the launch traced here: 26.5 us
  starting transfers between devices  12.4 us (46%)
  waiting for transfers between devices  11 us (41%)
  Pallas kernels  3.11 us (12%)
    ppermute x8, starting transfers between devices, send(): return lax.ppermute(array, ('blk', 'team'), pairs)  12.4 us
    ppermute x8, waiting for transfers between devices, send(): return lax.ppermute(array, ('blk', 'team'), pairs)  11 us
    pallas_call x1, Pallas kernels, pack(): pl.pallas_call(partial(pack_kernel, width, pieces), out_shape=[jax.ShapeD...  1.14 us
    pallas_call x1, Pallas kernels, paired(): pl.pallas_call(finish_kernel, out_shape=shape(rows, 2 * width), in_specs=...  0.89 us
    pallas_call x1, Pallas kernels, paired(): pl.pallas_call(partial(attend_kernel, rows, len(keys)), out_shape=[shape(...  0.84 us
  transfers between devices with their start and end apart: 8, of which 6 were waited for; matrix products, arithmetic and copies ran while one was open for 0% of the time, Pallas kernels for 1%

profile of v1, /device:TPU:0, one launch (start us, length us, event | category | flops | bytes accessed | tf_op | source)
XLA Modules:
  0.0 26.5 jit_solution(14053613799838683911)
XLA Ops:
  0.0 1.1 %pack.1 = (bf16[96,640]{1,0:T(8,128)(2,1)S(1)}, bf16[96,640]{1,0:T(8,128)(2,1)S(1)}, bf16[144,640]{1,0:T(8,128)(2,1)S(1)}, bf16[48,640]{1,0:T(8,128)(2,1)S(1)}, bf16[48,640]{1,0:T(8,128)(2,1)S(1)}) custom-call(bf16[48,1280]{1,0:T(8,128)(2,1)} %refs_0_.1, bf16[48,1280]{1,0:T(8,128)(2,1)} %refs_1_.1, bf16[48,1280]{1,0:T(8,128)(2,1)} %refs_2_.1), custom_call_target="tpu_custom_call" | custom-call | tf_op jit(solution)/shard_map/pack/pallas_call | solution.py:128
  1.1 3.0 %collective-permute-start = (bf16[144,640]{1,0:T(8,128)(2,1)S(1)}, bf16[144,640]{1,0:T(8,128)(2,1)S(1)}, u32[]{:S(2)}, u32[]{:S(2)}) collective-permute-start(bf16[144,640]{1,0:T(8,128)(2,1)S(1)} %get-tuple-element.15), channel_id=1, source_target_pairs={{0,2},{2,0},{4,6},{6,4},{8,10},{10,8},{12,14},{14,12},{1,3},{3,1},... | collective-permute-start | bytes 552968 | tf_op jit(solution)/shard_map/ppermute | solution.py:230
  4.2 2.6 %collective-permute-start.2 = (bf16[96,640]{1,0:T(8,128)(2,1)S(1)}, bf16[96,640]{1,0:T(8,128)(2,1)S(1)}, u32[]{:S(2)}, u32[]{:S(2)}) collective-permute-start(bf16[96,640]{1,0:T(8,128)(2,1)S(1)} %get-tuple-element.16), channel_id=1, source_target_pairs={{0,10},{2,8},{4,14},{6,12},{8,2},{10,0},{12,6},{14,4},{1,11},{3,9}... | collective-permute-start | bytes 368648 | tf_op jit(solution)/shard_map/ppermute | solution.py:230
  6.7 0.0 collective-permute-start.1
  6.8 2.8 %collective-permute-start.4 = (bf16[48,640]{1,0:T(8,128)(2,1)S(1)}, bf16[48,640]{1,0:T(8,128)(2,1)S(1)}, u32[]{:S(2)}, u32[]{:S(2)}) collective-permute-start(bf16[48,640]{1,0:T(8,128)(2,1)S(1)} %get-tuple-element.18), channel_id=1, source_target_pairs={{0,6},{2,4},{4,2},{6,0},{8,14},{10,12},{12,10},{14,8},{1,7},{3,5},... | collective-permute-start | bytes 184328 | tf_op jit(solution)/shard_map/ppermute | solution.py:230
  9.6 0.4 %collective-permute-start.3 = (bf16[48,640]{1,0:T(8,128)(2,1)S(1)}, bf16[48,640]{1,0:T(8,128)(2,1)S(1)}, u32[]{:S(2)}, u32[]{:S(2)}) collective-permute-start(bf16[48,640]{1,0:T(8,128)(2,1)S(1)} %get-tuple-element.17.refs_4_), channel_id=1, source_target_pairs={{0,4},{2,6},{4,0},{6,2},{8,12},{10,14},{12,8},{14,10},{1,5},{3,7},... | collective-permute-start | bytes 184328 | tf_op jit(solution)/shard_map/ppermute | solution.py:230
  10.0 3.7 %collective-permute-done.4.refs_7_ = bf16[48,640]{1,0:T(8,128)(2,1)S(1)} collective-permute-done((bf16[48,640]{1,0:T(8,128)(2,1)S(1)}, bf16[48,640]{1,0:T(8,128)(2,1)S(1)}, u32[]{:S(2)}, u32[]{:S(2)}) %collective-permute-start.4) | collective-permute-done | bytes 61472 | tf_op jit(solution)/shard_map/ppermute | solution.py:230
  13.7 0.8 %collective-permute-done.3.refs_6_ = bf16[48,640]{1,0:T(8,128)(2,1)S(1)} collective-permute-done((bf16[48,640]{1,0:T(8,128)(2,1)S(1)}, bf16[48,640]{1,0:T(8,128)(2,1)S(1)}, u32[]{:S(2)}, u32[]{:S(2)}) %collective-permute-start.3) | collective-permute-done | bytes 61472 | tf_op jit(solution)/shard_map/ppermute | solution.py:230
  14.5 2.7 %collective-permute-done.2.refs_3_ = bf16[96,640]{1,0:T(8,128)(2,1)S(1)} collective-permute-done((bf16[96,640]{1,0:T(8,128)(2,1)S(1)}, bf16[96,640]{1,0:T(8,128)(2,1)S(1)}, u32[]{:S(2)}, u32[]{:S(2)}) %collective-permute-start.2) | collective-permute-done | bytes 122912 | tf_op jit(solution)/shard_map/ppermute | solution.py:230
  17.1 0.6 %collective-permute-done.1.refs_2_ = bf16[96,640]{1,0:T(8,128)(2,1)S(1)} collective-permute-done((bf16[96,640]{1,0:T(8,128)(2,1)S(1)}, bf16[96,640]{1,0:T(8,128)(2,1)S(1)}, u32[]{:S(2)}, u32[]{:S(2)}) %collective-permute-start.1) | collective-permute-done | bytes 122912 | tf_op jit(solution)/shard_map/ppermute | solution.py:230
  17.7 0.0 collective-permute-done.refs_1_.refs_5_
  17.7 0.8 %attend.1 = (bf16[48,768]{1,0:T(8,128)(2,1)S(1)}, bf16[48,768]{1,0:T(8,128)(2,1)S(1)}, bf16[48,768]{1,0:T(8,128)(2,1)S(1)}, bf16[48,768]{1,0:T(8,128)(2,1)S(1)}) custom-call(bf16[96,640]{1,0:T(8,128)(2,1)S(1)} %get-tuple-element.14.refs_0_, bf16[144,640]{1,0:T(8,128)(2,1)S(1)} %collective-permute-done.refs_1_.refs_5_, ...), custom_call_target="tpu_custom_call" | custom-call | tf_op jit(solution)/shard_map/attend/pallas_call | solution.py:251
  18.6 1.6 %collective-permute-start.5 = (bf16[48,768]{1,0:T(8,128)(2,1)S(1)}, bf16[48,768]{1,0:T(8,128)(2,1)S(1)}, u32[]{:S(2)}, u32[]{:S(2)}) collective-permute-start(bf16[48,768]{1,0:T(8,128)(2,1)S(1)} %get-tuple-element.19), channel_id=1, source_target_pairs={{0,2},{2,0},{4,6},{6,4},{8,10},{10,8},{12,14},{14,12},{1,3},{3,1},... | collective-permute-start | bytes 221192 | tf_op jit(solution)/shard_map/ppermute | solution.py:230
  20.1 0.7 %collective-permute-start.6 = (bf16[48,768]{1,0:T(8,128)(2,1)S(1)}, bf16[48,768]{1,0:T(8,128)(2,1)S(1)}, u32[]{:S(2)}, u32[]{:S(2)}) collective-permute-start(bf16[48,768]{1,0:T(8,128)(2,1)S(1)} %get-tuple-element.20), channel_id=1, source_target_pairs={{0,6},{2,4},{4,2},{6,0},{8,14},{10,12},{12,10},{14,8},{1,7},{3,5},... | collective-permute-start | bytes 221192 | tf_op jit(solution)/shard_map/ppermute | solution.py:230
  20.8 1.3 %collective-permute-start.7 = (bf16[48,768]{1,0:T(8,128)(2,1)S(1)}, bf16[48,768]{1,0:T(8,128)(2,1)S(1)}, u32[]{:S(2)}, u32[]{:S(2)}) collective-permute-start(bf16[48,768]{1,0:T(8,128)(2,1)S(1)} %get-tuple-element.22), channel_id=1, source_target_pairs={{0,4},{2,6},{4,0},{6,2},{8,12},{10,14},{12,8},{14,10},{1,5},{3,7},... | collective-permute-start | bytes 221192 | tf_op jit(solution)/shard_map/ppermute | solution.py:230
  22.1 1.7 %collective-permute-done.5.refs_0_ = bf16[48,768]{1,0:T(8,128)(2,1)S(1)} collective-permute-done((bf16[48,768]{1,0:T(8,128)(2,1)S(1)}, bf16[48,768]{1,0:T(8,128)(2,1)S(1)}, u32[]{:S(2)}, u32[]{:S(2)}) %collective-permute-start.5) | collective-permute-done | bytes 73760 | tf_op jit(solution)/shard_map/ppermute | solution.py:230
  23.8 1.6 %collective-permute-done.6.refs_1_ = bf16[48,768]{1,0:T(8,128)(2,1)S(1)} collective-permute-done((bf16[48,768]{1,0:T(8,128)(2,1)S(1)}, bf16[48,768]{1,0:T(8,128)(2,1)S(1)}, u32[]{:S(2)}, u32[]{:S(2)}) %collective-permute-start.6) | collective-permute-done | bytes 73760 | tf_op jit(solution)/shard_map/ppermute | solution.py:230
  25.4 0.2 merge.1.other_ref
  25.6 0.0 collective-permute-done.7.answer_ref
  25.7 0.9 %finish.1 = bf16[48,1280]{1,0:T(8,128)(2,1)} custom-call(bf16[48,640]{1,0:T(8,128)(2,1)S(1)} %merge.1.other_ref, bf16[48,768]{1,0:T(8,128)(2,1)S(1)} %get-tuple-element.21.own_ref, bf16[48,768]{1,0:T(8,128)(2,1)S(1)} %collective-permute-done.7.answer_ref), custom_call_target="tpu_custom_call" | custom-call | tf_op jit(solution)/shard_map/finish/pallas_call | solution.py:270
Async XLA Ops:
  1.1 16.6 %collective-permute-start = (bf16[144,640]{1,0:T(8,128)(2,1)S(1)}, bf16[144,640]{1,0:T(8,128)(2,1)S(1)}, u32[]{:S(2)}, u32[]{:S(2)}) collective-permute-start(bf16[144,640]{1,0:T(8,128)(2,1)S(1)} %get-tuple-element.15), channel_id=1, source_target_pairs={{0,2},{2,0},{4,6},{6,4},{8,10},{10,8},{12,14},{14,12},{1,3},{3,1},... | collective-permute-start | bytes 552968 | tf_op jit(solution)/shard_map/ppermute | solution.py:230
  4.2 13.0 %collective-permute-start.2 = (bf16[96,640]{1,0:T(8,128)(2,1)S(1)}, bf16[96,640]{1,0:T(8,128)(2,1)S(1)}, u32[]{:S(2)}, u32[]{:S(2)}) collective-permute-start(bf16[96,640]{1,0:T(8,128)(2,1)S(1)} %get-tuple-element.16), channel_id=1, source_target_pairs={{0,10},{2,8},{4,14},{6,12},{8,2},{10,0},{12,6},{14,4},{1,11},{3,9}... | collective-permute-start | bytes 368648 | tf_op jit(solution)/shard_map/ppermute | solution.py:230
  6.7 11.0 %collective-permute-start.1 = (bf16[96,640]{1,0:T(8,128)(2,1)S(1)}, bf16[96,640]{1,0:T(8,128)(2,1)S(1)}, u32[]{:S(2)}, u32[]{:S(2)}) collective-permute-start(bf16[96,640]{1,0:T(8,128)(2,1)S(1)} %get-tuple-element.14.refs_0_), channel_id=1, source_target_pairs={{0,8},{2,10},{4,12},{6,14},{8,0},{10,2},{12,4},{14,6},{1,9},{3,11}... | collective-permute-start | bytes 368648 | tf_op jit(solution)/shard_map/ppermute | solution.py:230
  6.8 6.9 %collective-permute-start.4 = (bf16[48,640]{1,0:T(8,128)(2,1)S(1)}, bf16[48,640]{1,0:T(8,128)(2,1)S(1)}, u32[]{:S(2)}, u32[]{:S(2)}) collective-permute-start(bf16[48,640]{1,0:T(8,128)(2,1)S(1)} %get-tuple-element.18), channel_id=1, source_target_pairs={{0,6},{2,4},{4,2},{6,0},{8,14},{10,12},{12,10},{14,8},{1,7},{3,5},... | collective-permute-start | bytes 184328 | tf_op jit(solution)/shard_map/ppermute | solution.py:230
  9.6 4.9 %collective-permute-start.3 = (bf16[48,640]{1,0:T(8,128)(2,1)S(1)}, bf16[48,640]{1,0:T(8,128)(2,1)S(1)}, u32[]{:S(2)}, u32[]{:S(2)}) collective-permute-start(bf16[48,640]{1,0:T(8,128)(2,1)S(1)} %get-tuple-element.17.refs_4_), channel_id=1, source_target_pairs={{0,4},{2,6},{4,0},{6,2},{8,12},{10,14},{12,8},{14,10},{1,5},{3,7},... | collective-permute-start | bytes 184328 | tf_op jit(solution)/shard_map/ppermute | solution.py:230
  18.6 5.2 %collective-permute-start.5 = (bf16[48,768]{1,0:T(8,128)(2,1)S(1)}, bf16[48,768]{1,0:T(8,128)(2,1)S(1)}, u32[]{:S(2)}, u32[]{:S(2)}) collective-permute-start(bf16[48,768]{1,0:T(8,128)(2,1)S(1)} %get-tuple-element.19), channel_id=1, source_target_pairs={{0,2},{2,0},{4,6},{6,4},{8,10},{10,8},{12,14},{14,12},{1,3},{3,1},... | collective-permute-start | bytes 221192 | tf_op jit(solution)/shard_map/ppermute | solution.py:230
  20.1 5.3 %collective-permute-start.6 = (bf16[48,768]{1,0:T(8,128)(2,1)S(1)}, bf16[48,768]{1,0:T(8,128)(2,1)S(1)}, u32[]{:S(2)}, u32[]{:S(2)}) collective-permute-start(bf16[48,768]{1,0:T(8,128)(2,1)S(1)} %get-tuple-element.20), channel_id=1, source_target_pairs={{0,6},{2,4},{4,2},{6,0},{8,14},{10,12},{12,10},{14,8},{1,7},{3,5},... | collective-permute-start | bytes 221192 | tf_op jit(solution)/shard_map/ppermute | solution.py:230
  20.8 4.8 %collective-permute-start.7 = (bf16[48,768]{1,0:T(8,128)(2,1)S(1)}, bf16[48,768]{1,0:T(8,128)(2,1)S(1)}, u32[]{:S(2)}, u32[]{:S(2)}) collective-permute-start(bf16[48,768]{1,0:T(8,128)(2,1)S(1)} %get-tuple-element.22), channel_id=1, source_target_pairs={{0,4},{2,6},{4,0},{6,2},{8,12},{10,14},{12,8},{14,10},{1,5},{3,7},... | collective-permute-start | bytes 221192 | tf_op jit(solution)/shard_map/ppermute | solution.py:230

commit v2 on v1

--- a/solution.py
+++ b/solution.py
@@ -143,27 +143,40 @@
     n_queries = len(rest) // 2
     q_refs, o_refs = rest[:n_queries], rest[n_queries:]
     width = q_refs[0].shape[1]
-    scale = 1.0 / math.sqrt(HD)
+    scale = math.log2(math.e) / math.sqrt(HD)
     lane = lax.broadcasted_iota(jnp.int32, (n_queries * rows, HD), 1)
     slot, part = lax.rem(lane, GAP), lax.div(lane, GAP)
     stats = jnp.zeros((n_queries * rows, HD), jnp.float32)
-    for h in range(width // HD):
+
+    def load(refs, low, h):
         columns = slice(h * HD, (h + 1) * HD)
-        q = jnp.concatenate([ref[ref.shape[0] - rows :, columns] for ref in q_refs], axis=0)
-        k = jnp.concatenate([ref[:rows, columns] for ref in kv_refs], axis=0)
-        v = jnp.concatenate([ref[rows : 2 * rows, columns] for ref in kv_refs], axis=0)
-        scores = (
-            lax.dot_general(q, k, (((1,), (1,)), ((), ())), preferred_element_type=jnp.float32)
-            * scale
+        return jnp.concatenate([r[low(r) : low(r) + rows, columns] for r in refs], axis=0)
+
+    def score(h):
+        q = load(q_refs, lambda r: r.shape[0] - rows, h)
+        k = load(kv_refs, lambda r: 0, h)
+        product = lax.dot_general(
+            q, k, (((1,), (1,)), ((), ())), preferred_element_type=jnp.float32
         )
+        return product * scale
+
+    def weigh(scores):
         top = jnp.max(scores, axis=1, keepdims=True)
-        weights = jnp.exp(scores - top)
-        total = jnp.sum(weights, axis=1, keepdims=True)
-        mixed = jnp.dot(weights.astype(jnp.bfloat16), v, preferred_element_type=jnp.float32)
-        mixed = mixed.astype(jnp.bfloat16)
-        stats = jnp.where(slot == h, jnp.where(part < TOPS, top, total), stats)
+        return top, jnp.exp2(scores - top).astype(jnp.bfloat16)
+
+    def mix(h, top, weights, stats):
+        v = load(kv_refs, lambda r: rows, h)
+        v = jnp.concatenate([v, jnp.ones_like(v)], axis=1)
+        mixed = jnp.dot(weights, v, preferred_element_type=jnp.float32)
         for i, ref in enumerate(o_refs):
-            ref[:, columns] = mixed[i * rows : (i + 1) * rows]
+            ref[:, h * HD : (h + 1) * HD] = mixed[i * rows : (i + 1) * rows, :HD].astype(ref.dtype)
+        return jnp.where(slot == h, jnp.where(part < TOPS, top, mixed[:, HD:]), stats)
+
+    heads = width // HD
+    scores = [score(h) for h in range(heads)]
+    pairs = [weigh(s) for s in scores]
+    for h, (top, weights) in enumerate(pairs):
+        stats = mix(h, top, weights, stats)
     first = stats.astype(jnp.bfloat16).astype(jnp.float32)
     left = stats - first
     second = left.astype(jnp.bfloat16).astype(jnp.float32)
@@ -186,7 +199,7 @@
     common = tops[0]
     for top in tops[1:]:
         common = jnp.maximum(common, top)
-    factors = [jnp.exp(top - common) for top in tops]
+    factors = [jnp.exp2(top - common) for top in tops]
     row_sum = sum(f * t for f, t in zip(factors, totals))
     factors = [f / row_sum for f in factors]
     for h in range(width // HD):

time: 26.7 us -> 26.4 us (0.989)
  Pallas kernels: 3.11 us -> 2.84 us
where the time goes in v2:
time: 26.4 us; the launch traced here: 26.3 us
  starting transfers between devices  12.4 us (47%)
  waiting for transfers between devices  11 us (42%)
  Pallas kernels  2.84 us (11%)
    ppermute x8, starting transfers between devices, send(): return lax.ppermute(array, ('blk', 'team'), pairs)  12.4 us
    ppermute x8, waiting for transfers between devices, send(): return lax.ppermute(array, ('blk', 'team'), pairs)  11 us
    pallas_call x1, Pallas kernels, pack(): pl.pallas_call(partial(pack_kernel, width, pieces), out_shape=[jax.ShapeD...  1.14 us
    pallas_call x1, Pallas kernels, paired(): pl.pallas_call(finish_kernel, out_shape=shape(rows, 2 * width), in_specs=...  0.89 us
    pallas_call x1, Pallas kernels, paired(): pl.pallas_call(partial(attend_kernel, rows, len(keys)), out_shape=[shape(...  0.57 us
  transfers between devices with their start and end apart: 8, of which 6 were waited for; matrix products, arithmetic and copies ran while one was open for 0% of the time, Pallas kernels for 1%

profile of v2, /device:TPU:0, one launch (start us, length us, event | category | flops | bytes accessed | tf_op | source)
XLA Modules:
  0.0 26.3 jit_solution(10339669987299125586)
XLA Ops:
  0.0 1.1 %pack.1 = (bf16[96,640]{1,0:T(8,128)(2,1)S(1)}, bf16[96,640]{1,0:T(8,128)(2,1)S(1)}, bf16[144,640]{1,0:T(8,128)(2,1)S(1)}, bf16[48,640]{1,0:T(8,128)(2,1)S(1)}, bf16[48,640]{1,0:T(8,128)(2,1)S(1)}) custom-call(bf16[48,1280]{1,0:T(8,128)(2,1)} %refs_0_.1, bf16[48,1280]{1,0:T(8,128)(2,1)} %refs_1_.1, bf16[48,1280]{1,0:T(8,128)(2,1)} %refs_2_.1), custom_call_target="tpu_custom_call" | custom-call | tf_op jit(solution)/shard_map/pack/pallas_call | solution.py:128
  1.1 3.0 %collective-permute-start = (bf16[144,640]{1,0:T(8,128)(2,1)S(1)}, bf16[144,640]{1,0:T(8,128)(2,1)S(1)}, u32[]{:S(2)}, u32[]{:S(2)}) collective-permute-start(bf16[144,640]{1,0:T(8,128)(2,1)S(1)} %get-tuple-element.15), channel_id=1, source_target_pairs={{0,2},{2,0},{4,6},{6,4},{8,10},{10,8},{12,14},{14,12},{1,3},{3,1},... | collective-permute-start | bytes 552968 | tf_op jit(solution)/shard_map/ppermute | solution.py:243
  4.2 2.6 %collective-permute-start.2 = (bf16[96,640]{1,0:T(8,128)(2,1)S(1)}, bf16[96,640]{1,0:T(8,128)(2,1)S(1)}, u32[]{:S(2)}, u32[]{:S(2)}) collective-permute-start(bf16[96,640]{1,0:T(8,128)(2,1)S(1)} %get-tuple-element.16), channel_id=1, source_target_pairs={{0,10},{2,8},{4,14},{6,12},{8,2},{10,0},{12,6},{14,4},{1,11},{3,9}... | collective-permute-start | bytes 368648 | tf_op jit(solution)/shard_map/ppermute | solution.py:243
  6.7 0.0 collective-permute-start.1
  6.8 2.8 %collective-permute-start.4 = (bf16[48,640]{1,0:T(8,128)(2,1)S(1)}, bf16[48,640]{1,0:T(8,128)(2,1)S(1)}, u32[]{:S(2)}, u32[]{:S(2)}) collective-permute-start(bf16[48,640]{1,0:T(8,128)(2,1)S(1)} %get-tuple-element.18), channel_id=1, source_target_pairs={{0,6},{2,4},{4,2},{6,0},{8,14},{10,12},{12,10},{14,8},{1,7},{3,5},... | collective-permute-start | bytes 184328 | tf_op jit(solution)/shard_map/ppermute | solution.py:243
  9.6 0.4 %collective-permute-start.3 = (bf16[48,640]{1,0:T(8,128)(2,1)S(1)}, bf16[48,640]{1,0:T(8,128)(2,1)S(1)}, u32[]{:S(2)}, u32[]{:S(2)}) collective-permute-start(bf16[48,640]{1,0:T(8,128)(2,1)S(1)} %get-tuple-element.17.refs_4_), channel_id=1, source_target_pairs={{0,4},{2,6},{4,0},{6,2},{8,12},{10,14},{12,8},{14,10},{1,5},{3,7},... | collective-permute-start | bytes 184328 | tf_op jit(solution)/shard_map/ppermute | solution.py:243
  10.0 3.7 %collective-permute-done.4.refs_7_ = bf16[48,640]{1,0:T(8,128)(2,1)S(1)} collective-permute-done((bf16[48,640]{1,0:T(8,128)(2,1)S(1)}, bf16[48,640]{1,0:T(8,128)(2,1)S(1)}, u32[]{:S(2)}, u32[]{:S(2)}) %collective-permute-start.4) | collective-permute-done | bytes 61472 | tf_op jit(solution)/shard_map/ppermute | solution.py:243
  13.7 0.8 %collective-permute-done.3.refs_6_ = bf16[48,640]{1,0:T(8,128)(2,1)S(1)} collective-permute-done((bf16[48,640]{1,0:T(8,128)(2,1)S(1)}, bf16[48,640]{1,0:T(8,128)(2,1)S(1)}, u32[]{:S(2)}, u32[]{:S(2)}) %collective-permute-start.3) | collective-permute-done | bytes 61472 | tf_op jit(solution)/shard_map/ppermute | solution.py:243
  14.5 2.7 %collective-permute-done.2.refs_3_ = bf16[96,640]{1,0:T(8,128)(2,1)S(1)} collective-permute-done((bf16[96,640]{1,0:T(8,128)(2,1)S(1)}, bf16[96,640]{1,0:T(8,128)(2,1)S(1)}, u32[]{:S(2)}, u32[]{:S(2)}) %collective-permute-start.2) | collective-permute-done | bytes 122912 | tf_op jit(solution)/shard_map/ppermute | solution.py:243
  17.1 0.6 %collective-permute-done.1.refs_2_ = bf16[96,640]{1,0:T(8,128)(2,1)S(1)} collective-permute-done((bf16[96,640]{1,0:T(8,128)(2,1)S(1)}, bf16[96,640]{1,0:T(8,128)(2,1)S(1)}, u32[]{:S(2)}, u32[]{:S(2)}) %collective-permute-start.1) | collective-permute-done | bytes 122912 | tf_op jit(solution)/shard_map/ppermute | solution.py:243
  17.7 0.0 collective-permute-done.refs_1_.refs_5_
  17.7 0.6 %attend.1 = (bf16[48,768]{1,0:T(8,128)(2,1)S(1)}, bf16[48,768]{1,0:T(8,128)(2,1)S(1)}, bf16[48,768]{1,0:T(8,128)(2,1)S(1)}, bf16[48,768]{1,0:T(8,128)(2,1)S(1)}) custom-call(bf16[96,640]{1,0:T(8,128)(2,1)S(1)} %get-tuple-element.14.refs_0_, bf16[144,640]{1,0:T(8,128)(2,1)S(1)} %collective-permute-done.refs_1_.refs_5_, ...), custom_call_target="tpu_custom_call" | custom-call | tf_op jit(solution)/shard_map/attend/pallas_call | solution.py:264
  18.3 1.6 %collective-permute-start.5 = (bf16[48,768]{1,0:T(8,128)(2,1)S(1)}, bf16[48,768]{1,0:T(8,128)(2,1)S(1)}, u32[]{:S(2)}, u32[]{:S(2)}) collective-permute-start(bf16[48,768]{1,0:T(8,128)(2,1)S(1)} %get-tuple-element.19), channel_id=1, source_target_pairs={{0,2},{2,0},{4,6},{6,4},{8,10},{10,8},{12,14},{14,12},{1,3},{3,1},... | collective-permute-start | bytes 221192 | tf_op jit(solution)/shard_map/ppermute | solution.py:243
  19.9 0.7 %collective-permute-start.6 = (bf16[48,768]{1,0:T(8,128)(2,1)S(1)}, bf16[48,768]{1,0:T(8,128)(2,1)S(1)}, u32[]{:S(2)}, u32[]{:S(2)}) collective-permute-start(bf16[48,768]{1,0:T(8,128)(2,1)S(1)} %get-tuple-element.20), channel_id=1, source_target_pairs={{0,6},{2,4},{4,2},{6,0},{8,14},{10,12},{12,10},{14,8},{1,7},{3,5},... | collective-permute-start | bytes 221192 | tf_op jit(solution)/shard_map/ppermute | solution.py:243
  20.6 1.3 %collective-permute-start.7 = (bf16[48,768]{1,0:T(8,128)(2,1)S(1)}, bf16[48,768]{1,0:T(8,128)(2,1)S(1)}, u32[]{:S(2)}, u32[]{:S(2)}) collective-permute-start(bf16[48,768]{1,0:T(8,128)(2,1)S(1)} %get-tuple-element.22), channel_id=1, source_target_pairs={{0,4},{2,6},{4,0},{6,2},{8,12},{10,14},{12,8},{14,10},{1,5},{3,7},... | collective-permute-start | bytes 221192 | tf_op jit(solution)/shard_map/ppermute | solution.py:243
  21.8 1.7 %collective-permute-done.5.refs_0_ = bf16[48,768]{1,0:T(8,128)(2,1)S(1)} collective-permute-done((bf16[48,768]{1,0:T(8,128)(2,1)S(1)}, bf16[48,768]{1,0:T(8,128)(2,1)S(1)}, u32[]{:S(2)}, u32[]{:S(2)}) %collective-permute-start.5) | collective-permute-done | bytes 73760 | tf_op jit(solution)/shard_map/ppermute | solution.py:243
  23.5 1.6 %collective-permute-done.6.refs_1_ = bf16[48,768]{1,0:T(8,128)(2,1)S(1)} collective-permute-done((bf16[48,768]{1,0:T(8,128)(2,1)S(1)}, bf16[48,768]{1,0:T(8,128)(2,1)S(1)}, u32[]{:S(2)}, u32[]{:S(2)}) %collective-permute-start.6) | collective-permute-done | bytes 73760 | tf_op jit(solution)/shard_map/ppermute | solution.py:243
  25.1 0.2 merge.1.other_ref
  25.4 0.0 collective-permute-done.7.answer_ref
  25.4 0.9 %finish.1 = bf16[48,1280]{1,0:T(8,128)(2,1)} custom-call(bf16[48,640]{1,0:T(8,128)(2,1)S(1)} %merge.1.other_ref, bf16[48,768]{1,0:T(8,128)(2,1)S(1)} %get-tuple-element.21.own_ref, bf16[48,768]{1,0:T(8,128)(2,1)S(1)} %collective-permute-done.7.answer_ref), custom_call_target="tpu_custom_call" | custom-call | tf_op jit(solution)/shard_map/finish/pallas_call | solution.py:283
Async XLA Ops:
  1.1 16.6 %collective-permute-start = (bf16[144,640]{1,0:T(8,128)(2,1)S(1)}, bf16[144,640]{1,0:T(8,128)(2,1)S(1)}, u32[]{:S(2)}, u32[]{:S(2)}) collective-permute-start(bf16[144,640]{1,0:T(8,128)(2,1)S(1)} %get-tuple-element.15), channel_id=1, source_target_pairs={{0,2},{2,0},{4,6},{6,4},{8,10},{10,8},{12,14},{14,12},{1,3},{3,1},... | collective-permute-start | bytes 552968 | tf_op jit(solution)/shard_map/ppermute | solution.py:243
  4.2 13.0 %collective-permute-start.2 = (bf16[96,640]{1,0:T(8,128)(2,1)S(1)}, bf16[96,640]{1,0:T(8,128)(2,1)S(1)}, u32[]{:S(2)}, u32[]{:S(2)}) collective-permute-start(bf16[96,640]{1,0:T(8,128)(2,1)S(1)} %get-tuple-element.16), channel_id=1, source_target_pairs={{0,10},{2,8},{4,14},{6,12},{8,2},{10,0},{12,6},{14,4},{1,11},{3,9}... | collective-permute-start | bytes 368648 | tf_op jit(solution)/shard_map/ppermute | solution.py:243
  6.7 11.0 %collective-permute-start.1 = (bf16[96,640]{1,0:T(8,128)(2,1)S(1)}, bf16[96,640]{1,0:T(8,128)(2,1)S(1)}, u32[]{:S(2)}, u32[]{:S(2)}) collective-permute-start(bf16[96,640]{1,0:T(8,128)(2,1)S(1)} %get-tuple-element.14.refs_0_), channel_id=1, source_target_pairs={{0,8},{2,10},{4,12},{6,14},{8,0},{10,2},{12,4},{14,6},{1,9},{3,11}... | collective-permute-start | bytes 368648 | tf_op jit(solution)/shard_map/ppermute | solution.py:243
  6.8 6.9 %collective-permute-start.4 = (bf16[48,640]{1,0:T(8,128)(2,1)S(1)}, bf16[48,640]{1,0:T(8,128)(2,1)S(1)}, u32[]{:S(2)}, u32[]{:S(2)}) collective-permute-start(bf16[48,640]{1,0:T(8,128)(2,1)S(1)} %get-tuple-element.18), channel_id=1, source_target_pairs={{0,6},{2,4},{4,2},{6,0},{8,14},{10,12},{12,10},{14,8},{1,7},{3,5},... | collective-permute-start | bytes 184328 | tf_op jit(solution)/shard_map/ppermute | solution.py:243
  9.6 4.9 %collective-permute-start.3 = (bf16[48,640]{1,0:T(8,128)(2,1)S(1)}, bf16[48,640]{1,0:T(8,128)(2,1)S(1)}, u32[]{:S(2)}, u32[]{:S(2)}) collective-permute-start(bf16[48,640]{1,0:T(8,128)(2,1)S(1)} %get-tuple-element.17.refs_4_), channel_id=1, source_target_pairs={{0,4},{2,6},{4,0},{6,2},{8,12},{10,14},{12,8},{14,10},{1,5},{3,7},... | collective-permute-start | bytes 184328 | tf_op jit(solution)/shard_map/ppermute | solution.py:243
  18.3 5.2 %collective-permute-start.5 = (bf16[48,768]{1,0:T(8,128)(2,1)S(1)}, bf16[48,768]{1,0:T(8,128)(2,1)S(1)}, u32[]{:S(2)}, u32[]{:S(2)}) collective-permute-start(bf16[48,768]{1,0:T(8,128)(2,1)S(1)} %get-tuple-element.19), channel_id=1, source_target_pairs={{0,2},{2,0},{4,6},{6,4},{8,10},{10,8},{12,14},{14,12},{1,3},{3,1},... | collective-permute-start | bytes 221192 | tf_op jit(solution)/shard_map/ppermute | solution.py:243
  19.9 5.3 %collective-permute-start.6 = (bf16[48,768]{1,0:T(8,128)(2,1)S(1)}, bf16[48,768]{1,0:T(8,128)(2,1)S(1)}, u32[]{:S(2)}, u32[]{:S(2)}) collective-permute-start(bf16[48,768]{1,0:T(8,128)(2,1)S(1)} %get-tuple-element.20), channel_id=1, source_target_pairs={{0,6},{2,4},{4,2},{6,0},{8,14},{10,12},{12,10},{14,8},{1,7},{3,5},... | collective-permute-start | bytes 221192 | tf_op jit(solution)/shard_map/ppermute | solution.py:243
  20.6 4.8 %collective-permute-start.7 = (bf16[48,768]{1,0:T(8,128)(2,1)S(1)}, bf16[48,768]{1,0:T(8,128)(2,1)S(1)}, u32[]{:S(2)}, u32[]{:S(2)}) collective-permute-start(bf16[48,768]{1,0:T(8,128)(2,1)S(1)} %get-tuple-element.22), channel_id=1, source_target_pairs={{0,4},{2,6},{4,0},{6,2},{8,12},{10,14},{12,8},{14,10},{1,5},{3,7},... | collective-permute-start | bytes 221192 | tf_op jit(solution)/shard_map/ppermute | solution.py:243

commit v3 on v2

--- a/solution.py
+++ b/solution.py
@@ -138,23 +138,20 @@
     )(*map(hbm_array, arrays))
 
 
-def attend_kernel(rows, n_keys, *refs):
-    kv_refs, rest = refs[:n_keys], refs[n_keys:]
-    n_queries = len(rest) // 2
-    q_refs, o_refs = rest[:n_queries], rest[n_queries:]
-    width = q_refs[0].shape[1]
+def attend_kernel(rows, k_at, v_at, q_at, *refs):
+    o_refs = refs[-len(q_at) :]
+    width = o_refs[0].shape[1] - HD
     scale = math.log2(math.e) / math.sqrt(HD)
-    lane = lax.broadcasted_iota(jnp.int32, (n_queries * rows, HD), 1)
+    lane = lax.broadcasted_iota(jnp.int32, (len(q_at) * rows, HD), 1)
     slot, part = lax.rem(lane, GAP), lax.div(lane, GAP)
-    stats = jnp.zeros((n_queries * rows, HD), jnp.float32)
-
-    def load(refs, low, h):
+    stats = jnp.zeros(lane.shape, jnp.float32)
+
+    def load(places, h):
         columns = slice(h * HD, (h + 1) * HD)
-        return jnp.concatenate([r[low(r) : low(r) + rows, columns] for r in refs], axis=0)
+        return jnp.concatenate([refs[i][row : row + rows, columns] for i, row in places], axis=0)
 
     def score(h):
-        q = load(q_refs, lambda r: r.shape[0] - rows, h)
-        k = load(kv_refs, lambda r: 0, h)
+        q, k = load(q_at, h), load(k_at, h)
         product = lax.dot_general(
             q, k, (((1,), (1,)), ((), ())), preferred_element_type=jnp.float32
         )
@@ -165,7 +162,7 @@
         return top, jnp.exp2(scores - top).astype(jnp.bfloat16)
 
     def mix(h, top, weights, stats):
-        v = load(kv_refs, lambda r: rows, h)
+        v = load(v_at, h)
         v = jnp.concatenate([v, jnp.ones_like(v)], axis=1)
         mixed = jnp.dot(weights, v, preferred_element_type=jnp.float32)
         for i, ref in enumerate(o_refs):
@@ -185,6 +182,18 @@
     stats = stats.astype(jnp.bfloat16)
     for i, ref in enumerate(o_refs):
         ref[:, width:] = stats[i * rows : (i + 1) * rows]
+
+
+def split_kernel(*refs):
+    n_others = sum(ref.shape[1] == refs[-1].shape[1] for ref in refs) - 2
+    whole_refs, (keys_ref, queries_ref, *other_refs) = refs[: -2 - n_others], refs[-2 - n_others :]
+    rows, width = queries_ref.shape
+    own = lax.rem(lax.axis_index("team"), 2)
+    halves = [pl.ds(pl.multiple_of(half * width, HD), width) for half in (own, 1 - own)]
+    queries_ref[...] = whole_refs[-1][:, halves[0]]
+    for m, out_ref in enumerate((keys_ref, *other_refs)):
+        for i, whole_ref in enumerate(whole_refs[: out_ref.shape[0] // rows]):
+            out_ref[i * rows : (i + 1) * rows] = whole_ref[:, halves[m % 2]]
 
 
 def merge_kernel(*refs):
@@ -242,33 +251,52 @@
         ]
         return lax.ppermute(array, ("blk", "team"), pairs)
 
-    kv_own, kv_other, kvq_other, q_own, q_other = pack(
+    far = range(2, planes, 2)
+    whole = [send(key_rows, p, 0) for p in far] + [send(queries, 1, 0)]
+    kv_own, kvq_other, v_own, v_other, q_own, *kv_other = pack(
         (
             ((0, 0), (1, 0)),
-            ((0, 1), (1, 1)),
             ((0, 1), (1, 1), (2, 1)),
+            ((1, 0),),
+            ((1, 1),),
             ((2, 0),),
-            ((2, 1),),
+            *([((0, 1), (1, 1))] if members > 2 else []),
         ),
         key_rows,
         value_rows,
         queries,
     )
-
     near = send(kvq_other, 0, 1)
-    keys = [kv_own, near]
-    for plane_bits, member_bits in key_sends(planes, members):
-        array = kv_other if member_bits % 2 else kv_own
-        keys.append(send(array, plane_bits, member_bits))
-    asked = [q_own, near, send(q_own, 1, 0), send(q_other, 1, 1)]
+    beside = [kv_own, near]
+    beside += [send(kv_other[0] if m % 2 else kv_own, 0, m) for m in range(2, members)]
+    k_parts, v_parts = [(piece, 0) for piece in beside], [(piece, rows) for piece in beside]
+    v_parts += [(send(v_other if m % 2 else v_own, p, m), 0) for p in far for m in range(members)]
+    far_rows = len(far) * rows
+    mine, asked, *theirs = pl.pallas_call(
+        split_kernel,
+        out_shape=[shape(max(far_rows, rows), width), shape(rows, width)]
+        + [shape(far_rows + (rows if m == 1 else 0), width) for m in range(1, members)],
+        in_specs=[vmem_spec()] * len(whole),
+        out_specs=[vmem_spec()] * (1 + members),
+        compiler_params=params(),
+        name="split",
+    )(*whole)
+    shared = [mine] + [send(theirs[m - 1], 0, m) for m in range(1, members)]
+    k_parts += [(piece, i * rows) for piece in shared for i in range(len(far))]
+    q_parts = [(q_own, 0), (near, 2 * rows), (asked, 0), (shared[1], far_rows)]
+    operands = list({id(piece): piece for piece, _ in k_parts + v_parts + q_parts}.values())
+    place = {id(piece): i for i, piece in enumerate(operands)}
+    k_at, v_at, q_at = (
+        [(place[id(piece)], row) for piece, row in parts] for parts in (k_parts, v_parts, q_parts)
+    )
     own, *answers = pl.pallas_call(
-        partial(attend_kernel, rows, len(keys)),
-        out_shape=[shape(rows, width + HD)] * len(asked),
-        in_specs=[vmem_spec()] * (len(keys) + len(asked)),
-        out_specs=[vmem_spec()] * len(asked),
+        partial(attend_kernel, rows, k_at, v_at, q_at),
+        out_shape=[shape(rows, width + HD)] * len(q_at),
+        in_specs=[vmem_spec()] * len(operands),
+        out_specs=[vmem_spec()] * len(q_at),
         compiler_params=params(),
         name="attend",
-    )(*keys, *asked)
+    )(*operands)
     back_near = send(answers[0], 0, 1)
     back_ask = send(answers[1], 1, 0)
     back_cross = send(answers[2], 1, 1)
@@ -291,14 +319,10 @@
     )(early, own, back_ask)
 
 
-def key_sends(planes, members):
-    return [(p, m) for p in range(0, planes, 2) for m in range(members) if p or m > 1]
-
-
 def solution(mesh):
     spec = P(("groups", "blk", "team"), "head")
     planes, members = mesh.shape["blk"], mesh.shape["team"]
-    in_quads = all(n > 1 and n & (n - 1) == 0 for n in (planes, members))
+    in_quads = planes > 2 and members > 1 and all(n & (n - 1) == 0 for n in (planes, members))
 
     def local(queries, key_rows, value_rows):
         heads = queries.shape[1] // HD

time: 26.4 us -> 29.8 us (1.13)
  starting transfers between devices: 12.4 us -> 15.3 us
  waiting for transfers between devices: 11 us -> 11.5 us
    ppermute x8 -> x9, starting transfers between devices: 12.4 us -> 15.3 us  [send(): return lax.ppermute(array, ('blk', 'team'), pairs)]
    ppermute x8 -> x9, waiting for transfers between devices: 11 us -> 11.5 us  [send(): return lax.ppermute(array, ('blk', 'team'), pairs)]
  transfers between devices with their start and end apart: 8 -> 9, of which waited for: 6 -> 6; matrix products, arithmetic and copies ran while one was open for 0% -> 0% of each run, Pallas kernels for 1% -> 5%
where the time goes in v3:
time: 29.8 us; the launch traced here: 29.6 us
  starting transfers between devices  15.3 us (51%)
  waiting for transfers between devices  11.5 us (39%)
  Pallas kernels  2.82 us (9%)
    ppermute x9, starting transfers between devices, send(): return lax.ppermute(array, ('blk', 'team'), pairs)  15.3 us
    ppermute x9, waiting for transfers between devices, send(): return lax.ppermute(array, ('blk', 'team'), pairs)  11.5 us
    pallas_call x1, Pallas kernels, pack(): pl.pallas_call(partial(pack_kernel, width, pieces), out_shape=[jax.ShapeD...  1.1 us
    pallas_call x1, Pallas kernels, paired(): pl.pallas_call(finish_kernel, out_shape=shape(rows, 2 * width), in_specs=...  0.89 us
  transfers between devices with their start and end apart: 9, of which 6 were waited for; matrix products, arithmetic and copies ran while one was open for 0% of the time, Pallas kernels for 5%

profile of v3, /device:TPU:0, one launch (start us, length us, event | category | flops | bytes accessed | tf_op | source)
XLA Modules:
  0.0 29.6 jit_solution(1027551270797696647)
XLA Ops:
  0.0 3.1 %collective-permute-start.2 = (bf16[48,1280]{1,0:T(8,128)(2,1)}, bf16[48,1280]{1,0:T(8,128)(2,1)S(1)}, u32[]{:S(2)}, u32[]{:S(2)}) collective-permute-start(bf16[48,1280]{1,0:T(8,128)(2,1)} %refs_2_.1), channel_id=1, source_target_pairs={{0,4},{2,6},{4,0},{6,2},{8,12},{10,14},{12,8},{14,10},{1,5},{3,7},... | collective-permute-start | bytes 368648 | tf_op jit(solution)/shard_map/ppermute | solution.py:252
  3.1 2.6 %collective-permute-start.1 = (bf16[48,1280]{1,0:T(8,128)(2,1)}, bf16[48,1280]{1,0:T(8,128)(2,1)S(1)}, u32[]{:S(2)}, u32[]{:S(2)}) collective-permute-start(bf16[48,1280]{1,0:T(8,128)(2,1)} %refs_0_.1), channel_id=1, source_target_pairs={{0,8},{2,10},{4,12},{6,14},{8,0},{10,2},{12,4},{14,6},{1,9},{3,11}... | collective-permute-start | bytes 368648 | tf_op jit(solution)/shard_map/ppermute | solution.py:252
  5.6 1.1 %pack.1 = (bf16[96,640]{1,0:T(8,128)(2,1)S(1)}, bf16[144,640]{1,0:T(8,128)(2,1)S(1)}, bf16[48,640]{1,0:T(8,128)(2,1)S(1)}, bf16[48,640]{1,0:T(8,128)(2,1)S(1)}, bf16[48,640]{1,0:T(8,128)(2,1)S(1)}) custom-call(bf16[48,1280]{1,0:T(8,128)(2,1)} %refs_0_.1, bf16[48,1280]{1,0:T(8,128)(2,1)} %refs_1_.1, bf16[48,1280]{1,0:T(8,128)(2,1)} %refs_2_.1), custom_call_target="tpu_custom_call" | custom-call | tf_op jit(solution)/shard_map/pack/pallas_call | solution.py:128
  6.8 1.6 %collective-permute-start = (bf16[144,640]{1,0:T(8,128)(2,1)S(1)}, bf16[144,640]{1,0:T(8,128)(2,1)S(1)}, u32[]{:S(2)}, u32[]{:S(2)}) collective-permute-start(bf16[144,640]{1,0:T(8,128)(2,1)S(1)} %get-tuple-element.18), channel_id=1, source_target_pairs={{0,2},{2,0},{4,6},{6,4},{8,10},{10,8},{12,14},{14,12},{1,3},{3,1},... | collective-permute-start | bytes 552968 | tf_op jit(solution)/shard_map/ppermute | solution.py:252
  8.3 0.0 collective-permute-done.2.refs_1_
  8.3 3.3 %collective-permute-done.1.refs_0_ = bf16[48,1280]{1,0:T(8,128)(2,1)S(1)} collective-permute-done((bf16[48,1280]{1,0:T(8,128)(2,1)}, bf16[48,1280]{1,0:T(8,128)(2,1)S(1)}, u32[]{:S(2)}, u32[]{:S(2)}) %collective-permute-start.1) | collective-permute-done | bytes 122912 | tf_op jit(solution)/shard_map/ppermute | solution.py:252
  11.7 1.6 %collective-permute-start.3 = (bf16[96,640]{1,0:T(8,128)(2,1)S(1)}, bf16[96,640]{1,0:T(8,128)(2,1)S(1)}, u32[]{:S(2)}, u32[]{:S(2)}) collective-permute-start(bf16[96,640]{1,0:T(8,128)(2,1)S(1)} %get-tuple-element.20), channel_id=1, source_target_pairs={{0,2},{2,0},{4,6},{6,4},{8,10},{10,8},{12,14},{14,12},{1,3},{3,1},... | collective-permute-start | bytes 368648 | tf_op jit(solution)/shard_map/ppermute | solution.py:252
  13.2 0.3 %collective-permute-start.4 = (bf16[48,640]{1,0:T(8,128)(2,1)S(1)}, bf16[48,640]{1,0:T(8,128)(2,1)S(1)}, u32[]{:S(2)}, u32[]{:S(2)}) collective-permute-start(bf16[48,640]{1,0:T(8,128)(2,1)S(1)} %get-tuple-element.21), channel_id=1, source_target_pairs={{0,8},{2,10},{4,12},{6,14},{8,0},{10,2},{12,4},{14,6},{1,9},{3,11}... | collective-permute-start | bytes 184328 | tf_op jit(solution)/shard_map/ppermute | solution.py:252
  13.5 2.6 %collective-permute-start.5 = (bf16[48,640]{1,0:T(8,128)(2,1)S(1)}, bf16[48,640]{1,0:T(8,128)(2,1)S(1)}, u32[]{:S(2)}, u32[]{:S(2)}) collective-permute-start(bf16[48,640]{1,0:T(8,128)(2,1)S(1)} %get-tuple-element.22), channel_id=1, source_target_pairs={{0,10},{2,8},{4,14},{6,12},{8,2},{10,0},{12,6},{14,4},{1,11},{3,9}... | collective-permute-start | bytes 184328 | tf_op jit(solution)/shard_map/ppermute | solution.py:252
  16.1 3.4 %collective-permute-done.4.refs_4_ = bf16[48,640]{1,0:T(8,128)(2,1)S(1)} collective-permute-done((bf16[48,640]{1,0:T(8,128)(2,1)S(1)}, bf16[48,640]{1,0:T(8,128)(2,1)S(1)}, u32[]{:S(2)}, u32[]{:S(2)}) %collective-permute-start.4) | collective-permute-done | bytes 61472 | tf_op jit(solution)/shard_map/ppermute | solution.py:252
  19.5 0.7 %collective-permute-done.5.refs_5_ = bf16[48,640]{1,0:T(8,128)(2,1)S(1)} collective-permute-done((bf16[48,640]{1,0:T(8,128)(2,1)S(1)}, bf16[48,640]{1,0:T(8,128)(2,1)S(1)}, u32[]{:S(2)}, u32[]{:S(2)}) %collective-permute-start.5) | collective-permute-done | bytes 61472 | tf_op jit(solution)/shard_map/ppermute | solution.py:252
  20.2 0.0 collective-permute-done.refs_1_
  20.2 0.0 collective-permute-done.3.refs_3_
  20.2 0.6 %attend.1 = (bf16[48,768]{1,0:T(8,128)(2,1)S(1)}, bf16[48,768]{1,0:T(8,128)(2,1)S(1)}, bf16[48,768]{1,0:T(8,128)(2,1)S(1)}, bf16[48,768]{1,0:T(8,128)(2,1)S(1)}) custom-call(bf16[96,640]{1,0:T(8,128)(2,1)S(1)} %get-tuple-element.17.refs_0_, bf16[144,640]{1,0:T(8,128)(2,1)S(1)} %collective-permute-done.refs_1_, ...), custom_call_target="tpu_custom_call" | custom-call | tf_op jit(solution)/shard_map/attend/pallas_call | solution.py:292
  20.7 1.6 %collective-permute-start.6 = (bf16[48,768]{1,0:T(8,128)(2,1)S(1)}, bf16[48,768]{1,0:T(8,128)(2,1)S(1)}, u32[]{:S(2)}, u32[]{:S(2)}) collective-permute-start(bf16[48,768]{1,0:T(8,128)(2,1)S(1)} %get-tuple-element.25), channel_id=1, source_target_pairs={{0,2},{2,0},{4,6},{6,4},{8,10},{10,8},{12,14},{14,12},{1,3},{3,1},... | collective-permute-start | bytes 221192 | tf_op jit(solution)/shard_map/ppermute | solution.py:252
  22.3 2.0 %collective-permute-start.7 = (bf16[48,768]{1,0:T(8,128)(2,1)S(1)}, bf16[48,768]{1,0:T(8,128)(2,1)S(1)}, u32[]{:S(2)}, u32[]{:S(2)}) collective-permute-start(bf16[48,768]{1,0:T(8,128)(2,1)S(1)} %get-tuple-element.26), channel_id=1, source_target_pairs={{0,6},{2,4},{4,2},{6,0},{8,14},{10,12},{12,10},{14,8},{1,7},{3,5},... | collective-permute-start | bytes 221192 | tf_op jit(solution)/shard_map/ppermute | solution.py:252
  24.4 0.0 collective-permute-start.8
  24.4 0.8 %collective-permute-done.6.refs_0_ = bf16[48,768]{1,0:T(8,128)(2,1)S(1)} collective-permute-done((bf16[48,768]{1,0:T(8,128)(2,1)S(1)}, bf16[48,768]{1,0:T(8,128)(2,1)S(1)}, u32[]{:S(2)}, u32[]{:S(2)}) %collective-permute-start.6) | collective-permute-done | bytes 73760 | tf_op jit(solution)/shard_map/ppermute | solution.py:252
  25.2 2.4 %collective-permute-done.7.refs_1_ = bf16[48,768]{1,0:T(8,128)(2,1)S(1)} collective-permute-done((bf16[48,768]{1,0:T(8,128)(2,1)S(1)}, bf16[48,768]{1,0:T(8,128)(2,1)S(1)}, u32[]{:S(2)}, u32[]{:S(2)}) %collective-permute-start.7) | collective-permute-done | bytes 73760 | tf_op jit(solution)/shard_map/ppermute | solution.py:252
  27.6 0.2 merge.1.other_ref
  27.8 0.9 %collective-permute-done.8.answer_ref = bf16[48,768]{1,0:T(8,128)(2,1)S(1)} collective-permute-done((bf16[48,768]{1,0:T(8,128)(2,1)S(1)}, bf16[48,768]{1,0:T(8,128)(2,1)S(1)}, u32[]{:S(2)}, u32[]{:S(2)}) %collective-permute-start.8) | collective-permute-done | bytes 73760 | tf_op jit(solution)/shard_map/ppermute | solution.py:252
  28.7 0.9 %finish.1 = bf16[48,1280]{1,0:T(8,128)(2,1)} custom-call(bf16[48,640]{1,0:T(8,128)(2,1)S(1)} %merge.1.other_ref, bf16[48,768]{1,0:T(8,128)(2,1)S(1)} %get-tuple-element.27.own_ref, bf16[48,768]{1,0:T(8,128)(2,1)S(1)} %collective-permute-done.8.answer_ref), custom_call_target="tpu_custom_call" | custom-call | tf_op jit(solution)/shard_map/finish/pallas_call | solution.py:311
  (1 shorter events, 0.0 us)
Async XLA Ops:
  0.0 8.3 %collective-permute-start.2 = (bf16[48,1280]{1,0:T(8,128)(2,1)}, bf16[48,1280]{1,0:T(8,128)(2,1)S(1)}, u32[]{:S(2)}, u32[]{:S(2)}) collective-permute-start(bf16[48,1280]{1,0:T(8,128)(2,1)} %refs_2_.1), channel_id=1, source_target_pairs={{0,4},{2,6},{4,0},{6,2},{8,12},{10,14},{12,8},{14,10},{1,5},{3,7},... | collective-permute-start | bytes 368648 | tf_op jit(solution)/shard_map/ppermute | solution.py:252
  3.1 8.6 %collective-permute-start.1 = (bf16[48,1280]{1,0:T(8,128)(2,1)}, bf16[48,1280]{1,0:T(8,128)(2,1)S(1)}, u32[]{:S(2)}, u32[]{:S(2)}) collective-permute-start(bf16[48,1280]{1,0:T(8,128)(2,1)} %refs_0_.1), channel_id=1, source_target_pairs={{0,8},{2,10},{4,12},{6,14},{8,0},{10,2},{12,4},{14,6},{1,9},{3,11}... | collective-permute-start | bytes 368648 | tf_op jit(solution)/shard_map/ppermute | solution.py:252
  6.8 13.4 %collective-permute-start = (bf16[144,640]{1,0:T(8,128)(2,1)S(1)}, bf16[144,640]{1,0:T(8,128)(2,1)S(1)}, u32[]{:S(2)}, u32[]{:S(2)}) collective-permute-start(bf16[144,640]{1,0:T(8,128)(2,1)S(1)} %get-tuple-element.18), channel_id=1, source_target_pairs={{0,2},{2,0},{4,6},{6,4},{8,10},{10,8},{12,14},{14,12},{1,3},{3,1},... | collective-permute-start | bytes 552968 | tf_op jit(solution)/shard_map/ppermute | solution.py:252
  11.7 8.5 %collective-permute-start.3 = (bf16[96,640]{1,0:T(8,128)(2,1)S(1)}, bf16[96,640]{1,0:T(8,128)(2,1)S(1)}, u32[]{:S(2)}, u32[]{:S(2)}) collective-permute-start(bf16[96,640]{1,0:T(8,128)(2,1)S(1)} %get-tuple-element.20), channel_id=1, source_target_pairs={{0,2},{2,0},{4,6},{6,4},{8,10},{10,8},{12,14},{14,12},{1,3},{3,1},... | collective-permute-start | bytes 368648 | tf_op jit(solution)/shard_map/ppermute | solution.py:252
  13.2 6.3 %collective-permute-start.4 = (bf16[48,640]{1,0:T(8,128)(2,1)S(1)}, bf16[48,640]{1,0:T(8,128)(2,1)S(1)}, u32[]{:S(2)}, u32[]{:S(2)}) collective-permute-start(bf16[48,640]{1,0:T(8,128)(2,1)S(1)} %get-tuple-element.21), channel_id=1, source_target_pairs={{0,8},{2,10},{4,12},{6,14},{8,0},{10,2},{12,4},{14,6},{1,9},{3,11}... | collective-permute-start | bytes 184328 | tf_op jit(solution)/shard_map/ppermute | solution.py:252
  13.5 6.6 %collective-permute-start.5 = (bf16[48,640]{1,0:T(8,128)(2,1)S(1)}, bf16[48,640]{1,0:T(8,128)(2,1)S(1)}, u32[]{:S(2)}, u32[]{:S(2)}) collective-permute-start(bf16[48,640]{1,0:T(8,128)(2,1)S(1)} %get-tuple-element.22), channel_id=1, source_target_pairs={{0,10},{2,8},{4,14},{6,12},{8,2},{10,0},{12,6},{14,4},{1,11},{3,9}... | collective-permute-start | bytes 184328 | tf_op jit(solution)/shard_map/ppermute | solution.py:252
  20.7 4.4 %collective-permute-start.6 = (bf16[48,768]{1,0:T(8,128)(2,1)S(1)}, bf16[48,768]{1,0:T(8,128)(2,1)S(1)}, u32[]{:S(2)}, u32[]{:S(2)}) collective-permute-start(bf16[48,768]{1,0:T(8,128)(2,1)S(1)} %get-tuple-element.25), channel_id=1, source_target_pairs={{0,2},{2,0},{4,6},{6,4},{8,10},{10,8},{12,14},{14,12},{1,3},{3,1},... | collective-permute-start | bytes 221192 | tf_op jit(solution)/shard_map/ppermute | solution.py:252
  22.3 5.3 %collective-permute-start.7 = (bf16[48,768]{1,0:T(8,128)(2,1)S(1)}, bf16[48,768]{1,0:T(8,128)(2,1)S(1)}, u32[]{:S(2)}, u32[]{:S(2)}) collective-permute-start(bf16[48,768]{1,0:T(8,128)(2,1)S(1)} %get-tuple-element.26), channel_id=1, source_target_pairs={{0,6},{2,4},{4,2},{6,0},{8,14},{10,12},{12,10},{14,8},{1,7},{3,5},... | collective-permute-start | bytes 221192 | tf_op jit(solution)/shard_map/ppermute | solution.py:252
  24.4 4.4 %collective-permute-start.8 = (bf16[48,768]{1,0:T(8,128)(2,1)S(1)}, bf16[48,768]{1,0:T(8,128)(2,1)S(1)}, u32[]{:S(2)}, u32[]{:S(2)}) collective-permute-start(bf16[48,768]{1,0:T(8,128)(2,1)S(1)} %get-tuple-element.28), channel_id=1, source_target_pairs={{0,4},{2,6},{4,0},{6,2},{8,12},{10,14},{12,8},{14,10},{1,5},{3,7},... | collective-permute-start | bytes 221192 | tf_op jit(solution)/shard_map/ppermute | solution.py:252

commit v4 on v3

--- a/solution.py
+++ b/solution.py
@@ -184,16 +184,23 @@
         ref[:, width:] = stats[i * rows : (i + 1) * rows]
 
 
-def split_kernel(*refs):
-    n_others = sum(ref.shape[1] == refs[-1].shape[1] for ref in refs) - 2
-    whole_refs, (keys_ref, queries_ref, *other_refs) = refs[: -2 - n_others], refs[-2 - n_others :]
-    rows, width = queries_ref.shape
+def own_halves(width):
     own = lax.rem(lax.axis_index("team"), 2)
-    halves = [pl.ds(pl.multiple_of(half * width, HD), width) for half in (own, 1 - own)]
-    queries_ref[...] = whole_refs[-1][:, halves[0]]
-    for m, out_ref in enumerate((keys_ref, *other_refs)):
-        for i, whole_ref in enumerate(whole_refs[: out_ref.shape[0] // rows]):
+    return [pl.ds(pl.multiple_of(half * width, HD), width) for half in (own, 1 - own)]
+
+
+def split_keys_kernel(n_whole, *refs):
+    whole_refs, out_refs = refs[:n_whole], refs[n_whole:]
+    rows, halves = whole_refs[0].shape[0], own_halves(out_refs[0].shape[1])
+    for m, out_ref in enumerate(out_refs):
+        for i, whole_ref in enumerate(whole_refs):
             out_ref[i * rows : (i + 1) * rows] = whole_ref[:, halves[m % 2]]
+
+
+def join_queries_kernel(own_ref, whole_ref, out_ref):
+    rows, width = own_ref.shape
+    out_ref[:rows] = own_ref[...]
+    out_ref[rows:] = whole_ref[:, own_halves(width)[0]]
 
 
 def merge_kernel(*refs):
@@ -251,39 +258,42 @@
         ]
         return lax.ppermute(array, ("blk", "team"), pairs)
 
+    def small(kernel, shapes, *arrays):
+        return pl.pallas_call(
+            kernel,
+            out_shape=shapes,
+            in_specs=[vmem_spec()] * len(arrays),
+            out_specs=[vmem_spec()] * len(shapes),
+            compiler_params=params(),
+        )(*arrays)
+
     far = range(2, planes, 2)
-    whole = [send(key_rows, p, 0) for p in far] + [send(queries, 1, 0)]
-    kv_own, kvq_other, v_own, v_other, q_own, *kv_other = pack(
+    whole = [send(key_rows, p, 0) for p in far]
+    asked = send(queries, 0, 1)
+    kv_own, kv_other, v_own, v_other, q_own = pack(
         (
             ((0, 0), (1, 0)),
-            ((0, 1), (1, 1), (2, 1)),
+            ((0, 1), (1, 1)),
             ((1, 0),),
             ((1, 1),),
             ((2, 0),),
-            *([((0, 1), (1, 1))] if members > 2 else []),
         ),
         key_rows,
         value_rows,
         queries,
     )
-    near = send(kvq_other, 0, 1)
-    beside = [kv_own, near]
-    beside += [send(kv_other[0] if m % 2 else kv_own, 0, m) for m in range(2, members)]
+    beside = [kv_own, send(kv_other, 0, 1)]
+    beside += [send(kv_other if m % 2 else kv_own, 0, m) for m in range(2, members)]
     k_parts, v_parts = [(piece, 0) for piece in beside], [(piece, rows) for piece in beside]
     v_parts += [(send(v_other if m % 2 else v_own, p, m), 0) for p in far for m in range(members)]
-    far_rows = len(far) * rows
-    mine, asked, *theirs = pl.pallas_call(
-        split_kernel,
-        out_shape=[shape(max(far_rows, rows), width), shape(rows, width)]
-        + [shape(far_rows + (rows if m == 1 else 0), width) for m in range(1, members)],
-        in_specs=[vmem_spec()] * len(whole),
-        out_specs=[vmem_spec()] * (1 + members),
-        compiler_params=params(),
-        name="split",
-    )(*whole)
+    (joined,) = small(join_queries_kernel, [shape(2 * rows, width)], q_own, asked)
+    both = send(joined, 1, 0)
+    q_parts = [(joined, 0), (joined, rows), (both, 0), (both, rows)]
+    mine, *theirs = small(
+        partial(split_keys_kernel, len(whole)), [shape(len(far) * rows, width)] * members, *whole
+    )
     shared = [mine] + [send(theirs[m - 1], 0, m) for m in range(1, members)]
     k_parts += [(piece, i * rows) for piece in shared for i in range(len(far))]
-    q_parts = [(q_own, 0), (near, 2 * rows), (asked, 0), (shared[1], far_rows)]
     operands = list({id(piece): piece for piece, _ in k_parts + v_parts + q_parts}.values())
     place = {id(piece): i for i, piece in enumerate(operands)}
     k_at, v_at, q_at = (

time: 29.8 us -> 27.4 us (0.919)
  waiting for transfers between devices: 11.5 us -> 8.04 us
  starting transfers between devices: 15.3 us -> 16.3 us
    ppermute x9 -> x10, waiting for transfers between devices: 11.5 us -> 8.04 us  [send(): return lax.ppermute(array, ('blk', 'team'), pairs)]
    ppermute x9 -> x10, starting transfers between devices: 15.3 us -> 16.3 us  [send(): return lax.ppermute(array, ('blk', 'team'), pairs)]
  transfers between devices with their start and end apart: 9 -> 10, of which waited for: 6 -> 4; matrix products, arithmetic and copies ran while one was open for 0% -> 0% of each run, Pallas kernels for 5% -> 5%
where the time goes in v4:
time: 27.4 us; the launch traced here: 27.2 us
  starting transfers between devices  16.3 us (59%)
  waiting for transfers between devices  8.04 us (29%)
  Pallas kernels  2.79 us (10%)
    ppermute x10, starting transfers between devices, send(): return lax.ppermute(array, ('blk', 'team'), pairs)  16.3 us
    ppermute x10, waiting for transfers between devices, send(): return lax.ppermute(array, ('blk', 'team'), pairs)  8.04 us
    pallas_call x1, Pallas kernels, pack(): pl.pallas_call(partial(pack_kernel, width, pieces), out_shape=[jax.ShapeD...  1.06 us
    pallas_call x1, Pallas kernels, paired(): pl.pallas_call(finish_kernel, out_shape=shape(rows, 2 * width), in_specs=...  0.89 us
    pallas_call x1, Pallas kernels, paired(): pl.pallas_call(partial(attend_kernel, rows, k_at, v_at, q_at), out_shape=...  0.57 us
  transfers between devices with their start and end apart: 10, of which 4 were waited for; matrix products, arithmetic and copies ran while one was open for 0% of the time, Pallas kernels for 5%

profile of v4, /device:TPU:0, one launch (start us, length us, event | category | flops | bytes accessed | tf_op | source)
XLA Modules:
  0.0 27.2 jit_solution(13566701258850318229)
XLA Ops:
  0.0 3.0 %collective-permute-start.5 = (bf16[48,1280]{1,0:T(8,128)(2,1)}, bf16[48,1280]{1,0:T(8,128)(2,1)S(1)}, u32[]{:S(2)}, u32[]{:S(2)}) collective-permute-start(bf16[48,1280]{1,0:T(8,128)(2,1)} %refs_2_.1), channel_id=1, source_target_pairs={{0,2},{2,0},{4,6},{6,4},{8,10},{10,8},{12,14},{14,12},{1,3},{3,1},... | collective-permute-start | bytes 368648 | tf_op jit(solution)/shard_map/ppermute | solution.py:259
  3.0 2.6 %collective-permute-start.1 = (bf16[48,1280]{1,0:T(8,128)(2,1)}, bf16[48,1280]{1,0:T(8,128)(2,1)S(1)}, u32[]{:S(2)}, u32[]{:S(2)}) collective-permute-start(bf16[48,1280]{1,0:T(8,128)(2,1)} %refs_0_.1), channel_id=1, source_target_pairs={{0,8},{2,10},{4,12},{6,14},{8,0},{10,2},{12,4},{14,6},{1,9},{3,11}... | collective-permute-start | bytes 368648 | tf_op jit(solution)/shard_map/ppermute | solution.py:259
  5.6 1.1 %pack.1 = (bf16[96,640]{1,0:T(8,128)(2,1)S(1)}, bf16[96,640]{1,0:T(8,128)(2,1)S(1)}, bf16[48,640]{1,0:T(8,128)(2,1)S(1)}, bf16[48,640]{1,0:T(8,128)(2,1)S(1)}, bf16[48,640]{1,0:T(8,128)(2,1)S(1)}) custom-call(bf16[48,1280]{1,0:T(8,128)(2,1)} %refs_0_.1, bf16[48,1280]{1,0:T(8,128)(2,1)} %refs_1_.1, bf16[48,1280]{1,0:T(8,128)(2,1)} %refs_2_.1), custom_call_target="tpu_custom_call" | custom-call | tf_op jit(solution)/shard_map/pack/pallas_call | solution.py:128
  6.6 0.6 %collective-permute-start = (bf16[96,640]{1,0:T(8,128)(2,1)S(1)}, bf16[96,640]{1,0:T(8,128)(2,1)S(1)}, u32[]{:S(2)}, u32[]{:S(2)}) collective-permute-start(bf16[96,640]{1,0:T(8,128)(2,1)S(1)} %get-tuple-element.17), channel_id=1, source_target_pairs={{0,2},{2,0},{4,6},{6,4},{8,10},{10,8},{12,14},{14,12},{1,3},{3,1},... | collective-permute-start | bytes 368648 | tf_op jit(solution)/shard_map/ppermute | solution.py:259
  7.2 0.0 collective-permute-done.5.whole_ref
  7.3 1.6 %collective-permute-start.6 = (bf16[96,640]{1,0:T(8,128)(2,1)S(1)}, bf16[96,640]{1,0:T(8,128)(2,1)S(1)}, u32[]{:S(2)}, u32[]{:S(2)}) collective-permute-start(bf16[96,640]{1,0:T(8,128)(2,1)S(1)} %shard_map.38.refs_6_), channel_id=1, source_target_pairs={{0,4},{2,6},{4,0},{6,2},{8,12},{10,14},{12,8},{14,10},{1,5},{3,7},... | collective-permute-start | bytes 368648 | tf_op jit(solution)/shard_map/ppermute | solution.py:259
  8.9 2.5 %collective-permute-start.3 = (bf16[48,640]{1,0:T(8,128)(2,1)S(1)}, bf16[48,640]{1,0:T(8,128)(2,1)S(1)}, u32[]{:S(2)}, u32[]{:S(2)}) collective-permute-start(bf16[48,640]{1,0:T(8,128)(2,1)S(1)} %get-tuple-element.20), channel_id=1, source_target_pairs={{0,8},{2,10},{4,12},{6,14},{8,0},{10,2},{12,4},{14,6},{1,9},{3,11}... | collective-permute-start | bytes 184328 | tf_op jit(solution)/shard_map/ppermute | solution.py:259
  11.4 1.6 %collective-permute-start.4 = (bf16[48,640]{1,0:T(8,128)(2,1)S(1)}, bf16[48,640]{1,0:T(8,128)(2,1)S(1)}, u32[]{:S(2)}, u32[]{:S(2)}) collective-permute-start(bf16[48,640]{1,0:T(8,128)(2,1)S(1)} %get-tuple-element.21), channel_id=1, source_target_pairs={{0,10},{2,8},{4,14},{6,12},{8,2},{10,0},{12,6},{14,4},{1,11},{3,9}... | collective-permute-start | bytes 184328 | tf_op jit(solution)/shard_map/ppermute | solution.py:259
  13.1 0.0 collective-permute-done.1.refs_0_
  13.1 0.6 %collective-permute-start.2 = (bf16[48,640]{1,0:T(8,128)(2,1)S(1)}, bf16[48,640]{1,0:T(8,128)(2,1)S(1)}, u32[]{:S(2)}, u32[]{:S(2)}) collective-permute-start(bf16[48,640]{1,0:T(8,128)(2,1)S(1)} %get-tuple-element.19), channel_id=1, source_target_pairs={{0,2},{2,0},{4,6},{6,4},{8,10},{10,8},{12,14},{14,12},{1,3},{3,1},... | collective-permute-start | bytes 184328 | tf_op jit(solution)/shard_map/ppermute | solution.py:259
  13.7 1.0 %collective-permute-done.3.refs_4_ = bf16[48,640]{1,0:T(8,128)(2,1)S(1)} collective-permute-done((bf16[48,640]{1,0:T(8,128)(2,1)S(1)}, bf16[48,640]{1,0:T(8,128)(2,1)S(1)}, u32[]{:S(2)}, u32[]{:S(2)}) %collective-permute-start.3) | collective-permute-done | bytes 61472 | tf_op jit(solution)/shard_map/ppermute | solution.py:259
  14.7 3.3 %collective-permute-done.4.refs_5_ = bf16[48,640]{1,0:T(8,128)(2,1)S(1)} collective-permute-done((bf16[48,640]{1,0:T(8,128)(2,1)S(1)}, bf16[48,640]{1,0:T(8,128)(2,1)S(1)}, u32[]{:S(2)}, u32[]{:S(2)}) %collective-permute-start.4) | collective-permute-done | bytes 61472 | tf_op jit(solution)/shard_map/ppermute | solution.py:259
  18.0 0.0 collective-permute-done.refs_1_
  18.0 0.0 collective-permute-done.2.refs_3_
  18.0 0.0 collective-permute-done.6.refs_7_
  18.0 0.6 %attend.1 = (bf16[48,768]{1,0:T(8,128)(2,1)S(1)}, bf16[48,768]{1,0:T(8,128)(2,1)S(1)}, bf16[48,768]{1,0:T(8,128)(2,1)S(1)}, bf16[48,768]{1,0:T(8,128)(2,1)S(1)}) custom-call(bf16[96,640]{1,0:T(8,128)(2,1)S(1)} %get-tuple-element.16.refs_0_, bf16[96,640]{1,0:T(8,128)(2,1)S(1)} %collective-permute-done.refs_1_, bf16[48,640]{1,0:T(8,128)(2,1)S(1)} %get-tuple-element.18.refs_2_, ...), custom_call_target="tpu_custom_call" | custom-call | tf_op jit(solution)/shard_map/attend/pallas_call | solution.py:302
  18.6 2.2 %collective-permute-start.7 = (bf16[48,768]{1,0:T(8,128)(2,1)S(1)}, bf16[48,768]{1,0:T(8,128)(2,1)S(1)}, u32[]{:S(2)}, u32[]{:S(2)}) collective-permute-start(bf16[48,768]{1,0:T(8,128)(2,1)S(1)} %get-tuple-element.23), channel_id=1, source_target_pairs={{0,2},{2,0},{4,6},{6,4},{8,10},{10,8},{12,14},{14,12},{1,3},{3,1},... | collective-permute-start | bytes 221192 | tf_op jit(solution)/shard_map/ppermute | solution.py:259
  20.8 0.0 collective-permute-start.8
  20.8 1.5 %collective-permute-start.9 = (bf16[48,768]{1,0:T(8,128)(2,1)S(1)}, bf16[48,768]{1,0:T(8,128)(2,1)S(1)}, u32[]{:S(2)}, u32[]{:S(2)}) collective-permute-start(bf16[48,768]{1,0:T(8,128)(2,1)S(1)} %get-tuple-element.26), channel_id=1, source_target_pairs={{0,4},{2,6},{4,0},{6,2},{8,12},{10,14},{12,8},{14,10},{1,5},{3,7},... | collective-permute-start | bytes 221192 | tf_op jit(solution)/shard_map/ppermute | solution.py:259
  22.4 0.8 %collective-permute-done.7.refs_0_ = bf16[48,768]{1,0:T(8,128)(2,1)S(1)} collective-permute-done((bf16[48,768]{1,0:T(8,128)(2,1)S(1)}, bf16[48,768]{1,0:T(8,128)(2,1)S(1)}, u32[]{:S(2)}, u32[]{:S(2)}) %collective-permute-start.7) | collective-permute-done | bytes 73760 | tf_op jit(solution)/shard_map/ppermute | solution.py:259
  23.2 2.9 %collective-permute-done.8.refs_1_ = bf16[48,768]{1,0:T(8,128)(2,1)S(1)} collective-permute-done((bf16[48,768]{1,0:T(8,128)(2,1)S(1)}, bf16[48,768]{1,0:T(8,128)(2,1)S(1)}, u32[]{:S(2)}, u32[]{:S(2)}) %collective-permute-start.8) | collective-permute-done | bytes 73760 | tf_op jit(solution)/shard_map/ppermute | solution.py:259
  26.1 0.2 merge.1.other_ref
  26.3 0.0 collective-permute-done.9.answer_ref
  26.3 0.9 %finish.1 = bf16[48,1280]{1,0:T(8,128)(2,1)} custom-call(bf16[48,640]{1,0:T(8,128)(2,1)S(1)} %merge.1.other_ref, bf16[48,768]{1,0:T(8,128)(2,1)S(1)} %get-tuple-element.25.own_ref, bf16[48,768]{1,0:T(8,128)(2,1)S(1)} %collective-permute-done.9.answer_ref), custom_call_target="tpu_custom_call" | custom-call | tf_op jit(solution)/shard_map/finish/pallas_call | solution.py:321
  (2 shorter events, 0.0 us)
Async XLA Ops:
  0.0 7.2 %collective-permute-start.5 = (bf16[48,1280]{1,0:T(8,128)(2,1)}, bf16[48,1280]{1,0:T(8,128)(2,1)S(1)}, u32[]{:S(2)}, u32[]{:S(2)}) collective-permute-start(bf16[48,1280]{1,0:T(8,128)(2,1)} %refs_2_.1), channel_id=1, source_target_pairs={{0,2},{2,0},{4,6},{6,4},{8,10},{10,8},{12,14},{14,12},{1,3},{3,1},... | collective-permute-start | bytes 368648 | tf_op jit(solution)/shard_map/ppermute | solution.py:259
  3.0 10.1 %collective-permute-start.1 = (bf16[48,1280]{1,0:T(8,128)(2,1)}, bf16[48,1280]{1,0:T(8,128)(2,1)S(1)}, u32[]{:S(2)}, u32[]{:S(2)}) collective-permute-start(bf16[48,1280]{1,0:T(8,128)(2,1)} %refs_0_.1), channel_id=1, source_target_pairs={{0,8},{2,10},{4,12},{6,14},{8,0},{10,2},{12,4},{14,6},{1,9},{3,11}... | collective-permute-start | bytes 368648 | tf_op jit(solution)/shard_map/ppermute | solution.py:259
  6.6 11.4 %collective-permute-start = (bf16[96,640]{1,0:T(8,128)(2,1)S(1)}, bf16[96,640]{1,0:T(8,128)(2,1)S(1)}, u32[]{:S(2)}, u32[]{:S(2)}) collective-permute-start(bf16[96,640]{1,0:T(8,128)(2,1)S(1)} %get-tuple-element.17), channel_id=1, source_target_pairs={{0,2},{2,0},{4,6},{6,4},{8,10},{10,8},{12,14},{14,12},{1,3},{3,1},... | collective-permute-start | bytes 368648 | tf_op jit(solution)/shard_map/ppermute | solution.py:259
  7.3 10.8 %collective-permute-start.6 = (bf16[96,640]{1,0:T(8,128)(2,1)S(1)}, bf16[96,640]{1,0:T(8,128)(2,1)S(1)}, u32[]{:S(2)}, u32[]{:S(2)}) collective-permute-start(bf16[96,640]{1,0:T(8,128)(2,1)S(1)} %shard_map.38.refs_6_), channel_id=1, source_target_pairs={{0,4},{2,6},{4,0},{6,2},{8,12},{10,14},{12,8},{14,10},{1,5},{3,7},... | collective-permute-start | bytes 368648 | tf_op jit(solution)/shard_map/ppermute | solution.py:259
  8.9 5.8 %collective-permute-start.3 = (bf16[48,640]{1,0:T(8,128)(2,1)S(1)}, bf16[48,640]{1,0:T(8,128)(2,1)S(1)}, u32[]{:S(2)}, u32[]{:S(2)}) collective-permute-start(bf16[48,640]{1,0:T(8,128)(2,1)S(1)} %get-tuple-element.20), channel_id=1, source_target_pairs={{0,8},{2,10},{4,12},{6,14},{8,0},{10,2},{12,4},{14,6},{1,9},{3,11}... | collective-permute-start | bytes 184328 | tf_op jit(solution)/shard_map/ppermute | solution.py:259
  11.4 6.6 %collective-permute-start.4 = (bf16[48,640]{1,0:T(8,128)(2,1)S(1)}, bf16[48,640]{1,0:T(8,128)(2,1)S(1)}, u32[]{:S(2)}, u32[]{:S(2)}) collective-permute-start(bf16[48,640]{1,0:T(8,128)(2,1)S(1)} %get-tuple-element.21), channel_id=1, source_target_pairs={{0,10},{2,8},{4,14},{6,12},{8,2},{10,0},{12,6},{14,4},{1,11},{3,9}... | collective-permute-start | bytes 184328 | tf_op jit(solution)/shard_map/ppermute | solution.py:259
  13.1 5.0 %collective-permute-start.2 = (bf16[48,640]{1,0:T(8,128)(2,1)S(1)}, bf16[48,640]{1,0:T(8,128)(2,1)S(1)}, u32[]{:S(2)}, u32[]{:S(2)}) collective-permute-start(bf16[48,640]{1,0:T(8,128)(2,1)S(1)} %get-tuple-element.19), channel_id=1, source_target_pairs={{0,2},{2,0},{4,6},{6,4},{8,10},{10,8},{12,14},{14,12},{1,3},{3,1},... | collective-permute-start | bytes 184328 | tf_op jit(solution)/shard_map/ppermute | solution.py:259
  18.6 4.6 %collective-permute-start.7 = (bf16[48,768]{1,0:T(8,128)(2,1)S(1)}, bf16[48,768]{1,0:T(8,128)(2,1)S(1)}, u32[]{:S(2)}, u32[]{:S(2)}) collective-permute-start(bf16[48,768]{1,0:T(8,128)(2,1)S(1)} %get-tuple-element.23), channel_id=1, source_target_pairs={{0,2},{2,0},{4,6},{6,4},{8,10},{10,8},{12,14},{14,12},{1,3},{3,1},... | collective-permute-start | bytes 221192 | tf_op jit(solution)/shard_map/ppermute | solution.py:259
  20.8 5.3 %collective-permute-start.8 = (bf16[48,768]{1,0:T(8,128)(2,1)S(1)}, bf16[48,768]{1,0:T(8,128)(2,1)S(1)}, u32[]{:S(2)}, u32[]{:S(2)}) collective-permute-start(bf16[48,768]{1,0:T(8,128)(2,1)S(1)} %get-tuple-element.24), channel_id=1, source_target_pairs={{0,6},{2,4},{4,2},{6,0},{8,14},{10,12},{12,10},{14,8},{1,7},{3,5},... | collective-permute-start | bytes 221192 | tf_op jit(solution)/shard_map/ppermute | solution.py:259
  20.8 5.5 %collective-permute-start.9 = (bf16[48,768]{1,0:T(8,128)(2,1)S(1)}, bf16[48,768]{1,0:T(8,128)(2,1)S(1)}, u32[]{:S(2)}, u32[]{:S(2)}) collective-permute-start(bf16[48,768]{1,0:T(8,128)(2,1)S(1)} %get-tuple-element.26), channel_id=1, source_target_pairs={{0,4},{2,6},{4,0},{6,2},{8,12},{10,14},{12,8},{14,10},{1,5},{3,7},... | collective-permute-start | bytes 221192 | tf_op jit(solution)/shard_map/ppermute | solution.py:259

commit v5 on v4

--- a/solution.py
+++ b/solution.py
@@ -155,11 +155,11 @@
         product = lax.dot_general(
             q, k, (((1,), (1,)), ((), ())), preferred_element_type=jnp.float32
         )
-        return product * scale
+        return product
 
     def weigh(scores):
         top = jnp.max(scores, axis=1, keepdims=True)
-        return top, jnp.exp2(scores - top).astype(jnp.bfloat16)
+        return top * scale, jnp.exp2((scores - top) * scale).astype(jnp.bfloat16)
 
     def mix(h, top, weights, stats):
         v = load(v_at, h)
@@ -272,7 +272,7 @@
     asked = send(queries, 0, 1)
     kv_own, kv_other, v_own, v_other, q_own = pack(
         (
-            ((0, 0), (1, 0)),
+            ((0, 0),) if members == 2 else ((0, 0), (1, 0)),
             ((0, 1), (1, 1)),
             ((1, 0),),
             ((1, 1),),
@@ -285,6 +285,7 @@
     beside = [kv_own, send(kv_other, 0, 1)]
     beside += [send(kv_other if m % 2 else kv_own, 0, m) for m in range(2, members)]
     k_parts, v_parts = [(piece, 0) for piece in beside], [(piece, rows) for piece in beside]
+    v_parts[0] = (v_own, 0)
     v_parts += [(send(v_other if m % 2 else v_own, p, m), 0) for p in far for m in range(members)]
     (joined,) = small(join_queries_kernel, [shape(2 * rows, width)], q_own, asked)
     both = send(joined, 1, 0)

time: 27.4 us -> 27 us (0.985)
  transfers between devices with their start and end apart: 10 -> 10, of which waited for: 4 -> 5; matrix products, arithmetic and copies ran while one was open for 0% -> 0% of each run, Pallas kernels for 5% -> 5%
where the time goes in v5:
time: 27 us; the launch traced here: 26.9 us
  starting transfers between devices  16.2 us (60%)
  waiting for transfers between devices  7.89 us (29%)
  Pallas kernels  2.75 us (10%)
    ppermute x10, starting transfers between devices, send(): return lax.ppermute(array, ('blk', 'team'), pairs)  16.2 us
    ppermute x10, waiting for transfers between devices, send(): return lax.ppermute(array, ('blk', 'team'), pairs)  7.89 us
    pallas_call x1, Pallas kernels, pack(): pl.pallas_call(partial(pack_kernel, width, pieces), out_shape=[jax.ShapeD...  1.03 us
    pallas_call x1, Pallas kernels, paired(): pl.pallas_call(finish_kernel, out_shape=shape(rows, 2 * width), in_specs=...  0.89 us
    pallas_call x1, Pallas kernels, paired(): pl.pallas_call(partial(attend_kernel, rows, k_at, v_at, q_at), out_shape=...  0.57 us
  transfers between devices with their start and end apart: 10, of which 5 were waited for; matrix products, arithmetic and copies ran while one was open for 0% of the time, Pallas kernels for 5%

profile of v5, /device:TPU:0, one launch (start us, length us, event | category | flops | bytes accessed | tf_op | source)
XLA Modules:
  0.0 26.9 jit_solution(3286347528760021941)
XLA Ops:
  0.0 3.0 %collective-permute-start.5 = (bf16[48,1280]{1,0:T(8,128)(2,1)}, bf16[48,1280]{1,0:T(8,128)(2,1)S(1)}, u32[]{:S(2)}, u32[]{:S(2)}) collective-permute-start(bf16[48,1280]{1,0:T(8,128)(2,1)} %refs_2_.1), channel_id=1, source_target_pairs={{0,2},{2,0},{4,6},{6,4},{8,10},{10,8},{12,14},{14,12},{1,3},{3,1},... | collective-permute-start | bytes 368648 | tf_op jit(solution)/shard_map/ppermute | solution.py:259
  3.0 2.6 %collective-permute-start.1 = (bf16[48,1280]{1,0:T(8,128)(2,1)}, bf16[48,1280]{1,0:T(8,128)(2,1)S(1)}, u32[]{:S(2)}, u32[]{:S(2)}) collective-permute-start(bf16[48,1280]{1,0:T(8,128)(2,1)} %refs_0_.1), channel_id=1, source_target_pairs={{0,8},{2,10},{4,12},{6,14},{8,0},{10,2},{12,4},{14,6},{1,9},{3,11}... | collective-permute-start | bytes 368648 | tf_op jit(solution)/shard_map/ppermute | solution.py:259
  5.6 1.0 %pack.1 = (bf16[48,640]{1,0:T(8,128)(2,1)S(1)}, bf16[96,640]{1,0:T(8,128)(2,1)S(1)}, bf16[48,640]{1,0:T(8,128)(2,1)S(1)}, bf16[48,640]{1,0:T(8,128)(2,1)S(1)}, bf16[48,640]{1,0:T(8,128)(2,1)S(1)}) custom-call(bf16[48,1280]{1,0:T(8,128)(2,1)} %refs_0_.1, bf16[48,1280]{1,0:T(8,128)(2,1)} %refs_1_.1, bf16[48,1280]{1,0:T(8,128)(2,1)} %refs_2_.1), custom_call_target="tpu_custom_call" | custom-call | tf_op jit(solution)/shard_map/pack/pallas_call | solution.py:128
  6.6 0.6 %collective-permute-start = (bf16[96,640]{1,0:T(8,128)(2,1)S(1)}, bf16[96,640]{1,0:T(8,128)(2,1)S(1)}, u32[]{:S(2)}, u32[]{:S(2)}) collective-permute-start(bf16[96,640]{1,0:T(8,128)(2,1)S(1)} %get-tuple-element.17), channel_id=1, source_target_pairs={{0,2},{2,0},{4,6},{6,4},{8,10},{10,8},{12,14},{14,12},{1,3},{3,1},... | collective-permute-start | bytes 368648 | tf_op jit(solution)/shard_map/ppermute | solution.py:259
  7.2 0.0 collective-permute-done.5.whole_ref
  7.2 1.6 %collective-permute-start.6 = (bf16[96,640]{1,0:T(8,128)(2,1)S(1)}, bf16[96,640]{1,0:T(8,128)(2,1)S(1)}, u32[]{:S(2)}, u32[]{:S(2)}) collective-permute-start(bf16[96,640]{1,0:T(8,128)(2,1)S(1)} %shard_map.38.refs_7_), channel_id=1, source_target_pairs={{0,4},{2,6},{4,0},{6,2},{8,12},{10,14},{12,8},{14,10},{1,5},{3,7},... | collective-permute-start | bytes 368648 | tf_op jit(solution)/shard_map/ppermute | solution.py:259
  8.9 4.2 %collective-permute-start.4 = (bf16[48,640]{1,0:T(8,128)(2,1)S(1)}, bf16[48,640]{1,0:T(8,128)(2,1)S(1)}, u32[]{:S(2)}, u32[]{:S(2)}) collective-permute-start(bf16[48,640]{1,0:T(8,128)(2,1)S(1)} %get-tuple-element.21), channel_id=1, source_target_pairs={{0,10},{2,8},{4,14},{6,12},{8,2},{10,0},{12,6},{14,4},{1,11},{3,9}... | collective-permute-start | bytes 184328 | tf_op jit(solution)/shard_map/ppermute | solution.py:259
  13.1 0.0 collective-permute-start.3
  13.1 0.0 collective-permute-done.1.refs_0_
  13.1 0.6 %collective-permute-start.2 = (bf16[48,640]{1,0:T(8,128)(2,1)S(1)}, bf16[48,640]{1,0:T(8,128)(2,1)S(1)}, u32[]{:S(2)}, u32[]{:S(2)}) collective-permute-start(bf16[48,640]{1,0:T(8,128)(2,1)S(1)} %get-tuple-element.19), channel_id=1, source_target_pairs={{0,2},{2,0},{4,6},{6,4},{8,10},{10,8},{12,14},{14,12},{1,3},{3,1},... | collective-permute-start | bytes 184328 | tf_op jit(solution)/shard_map/ppermute | solution.py:259
  13.7 2.1 %collective-permute-done.4.refs_6_ = bf16[48,640]{1,0:T(8,128)(2,1)S(1)} collective-permute-done((bf16[48,640]{1,0:T(8,128)(2,1)S(1)}, bf16[48,640]{1,0:T(8,128)(2,1)S(1)}, u32[]{:S(2)}, u32[]{:S(2)}) %collective-permute-start.4) | collective-permute-done | bytes 61472 | tf_op jit(solution)/shard_map/ppermute | solution.py:259
  15.8 2.9 %collective-permute-done.3.refs_5_ = bf16[48,640]{1,0:T(8,128)(2,1)S(1)} collective-permute-done((bf16[48,640]{1,0:T(8,128)(2,1)S(1)}, bf16[48,640]{1,0:T(8,128)(2,1)S(1)}, u32[]{:S(2)}, u32[]{:S(2)}) %collective-permute-start.3) | collective-permute-done | bytes 61472 | tf_op jit(solution)/shard_map/ppermute | solution.py:259
  18.7 0.0 collective-permute-done.refs_1_
  18.7 0.0 collective-permute-done.2.refs_3_
  18.7 0.0 collective-permute-done.6.refs_8_
  18.7 0.6 %attend.1 = (bf16[48,768]{1,0:T(8,128)(2,1)S(1)}, bf16[48,768]{1,0:T(8,128)(2,1)S(1)}, bf16[48,768]{1,0:T(8,128)(2,1)S(1)}, bf16[48,768]{1,0:T(8,128)(2,1)S(1)}) custom-call(bf16[48,640]{1,0:T(8,128)(2,1)S(1)} %get-tuple-element.16.refs_0_, bf16[96,640]{1,0:T(8,128)(2,1)S(1)} %collective-permute-done.refs_1_, bf16[48,640]{1,0:T(8,128)(2,1)S(1)} %get-tuple-element.18.refs_2_, ...), custom_call_target="tpu_custom_call" | custom-call | tf_op jit(solution)/shard_map/attend/pallas_call | solution.py:303
  19.3 0.1 collective-permute-start.7
  19.4 1.4 %collective-permute-start.8 = (bf16[48,768]{1,0:T(8,128)(2,1)S(1)}, bf16[48,768]{1,0:T(8,128)(2,1)S(1)}, u32[]{:S(2)}, u32[]{:S(2)}) collective-permute-start(bf16[48,768]{1,0:T(8,128)(2,1)S(1)} %get-tuple-element.24), channel_id=1, source_target_pairs={{0,6},{2,4},{4,2},{6,0},{8,14},{10,12},{12,10},{14,8},{1,7},{3,5},... | collective-permute-start | bytes 221192 | tf_op jit(solution)/shard_map/ppermute | solution.py:259
  20.8 2.1 %collective-permute-start.9 = (bf16[48,768]{1,0:T(8,128)(2,1)S(1)}, bf16[48,768]{1,0:T(8,128)(2,1)S(1)}, u32[]{:S(2)}, u32[]{:S(2)}) collective-permute-start(bf16[48,768]{1,0:T(8,128)(2,1)S(1)} %get-tuple-element.26), channel_id=1, source_target_pairs={{0,4},{2,6},{4,0},{6,2},{8,12},{10,14},{12,8},{14,10},{1,5},{3,7},... | collective-permute-start | bytes 221192 | tf_op jit(solution)/shard_map/ppermute | solution.py:259
  22.9 0.9 %collective-permute-done.7.refs_0_ = bf16[48,768]{1,0:T(8,128)(2,1)S(1)} collective-permute-done((bf16[48,768]{1,0:T(8,128)(2,1)S(1)}, bf16[48,768]{1,0:T(8,128)(2,1)S(1)}, u32[]{:S(2)}, u32[]{:S(2)}) %collective-permute-start.7) | collective-permute-done | bytes 73760 | tf_op jit(solution)/shard_map/ppermute | solution.py:259
  23.7 1.0 %collective-permute-done.8.refs_1_ = bf16[48,768]{1,0:T(8,128)(2,1)S(1)} collective-permute-done((bf16[48,768]{1,0:T(8,128)(2,1)S(1)}, bf16[48,768]{1,0:T(8,128)(2,1)S(1)}, u32[]{:S(2)}, u32[]{:S(2)}) %collective-permute-start.8) | collective-permute-done | bytes 73760 | tf_op jit(solution)/shard_map/ppermute | solution.py:259
  24.7 0.2 merge.1.other_ref
  24.9 1.0 %collective-permute-done.9.answer_ref = bf16[48,768]{1,0:T(8,128)(2,1)S(1)} collective-permute-done((bf16[48,768]{1,0:T(8,128)(2,1)S(1)}, bf16[48,768]{1,0:T(8,128)(2,1)S(1)}, u32[]{:S(2)}, u32[]{:S(2)}) %collective-permute-start.9) | collective-permute-done | bytes 73760 | tf_op jit(solution)/shard_map/ppermute | solution.py:259
  26.0 0.9 %finish.1 = bf16[48,1280]{1,0:T(8,128)(2,1)} custom-call(bf16[48,640]{1,0:T(8,128)(2,1)S(1)} %merge.1.other_ref, bf16[48,768]{1,0:T(8,128)(2,1)S(1)} %get-tuple-element.25.own_ref, bf16[48,768]{1,0:T(8,128)(2,1)S(1)} %collective-permute-done.9.answer_ref), custom_call_target="tpu_custom_call" | custom-call | tf_op jit(solution)/shard_map/finish/pallas_call | solution.py:322
  (2 shorter events, 0.0 us)
Async XLA Ops:
  0.0 7.2 %collective-permute-start.5 = (bf16[48,1280]{1,0:T(8,128)(2,1)}, bf16[48,1280]{1,0:T(8,128)(2,1)S(1)}, u32[]{:S(2)}, u32[]{:S(2)}) collective-permute-start(bf16[48,1280]{1,0:T(8,128)(2,1)} %refs_2_.1), channel_id=1, source_target_pairs={{0,2},{2,0},{4,6},{6,4},{8,10},{10,8},{12,14},{14,12},{1,3},{3,1},... | collective-permute-start | bytes 368648 | tf_op jit(solution)/shard_map/ppermute | solution.py:259
  3.0 10.1 %collective-permute-start.1 = (bf16[48,1280]{1,0:T(8,128)(2,1)}, bf16[48,1280]{1,0:T(8,128)(2,1)S(1)}, u32[]{:S(2)}, u32[]{:S(2)}) collective-permute-start(bf16[48,1280]{1,0:T(8,128)(2,1)} %refs_0_.1), channel_id=1, source_target_pairs={{0,8},{2,10},{4,12},{6,14},{8,0},{10,2},{12,4},{14,6},{1,9},{3,11}... | collective-permute-start | bytes 368648 | tf_op jit(solution)/shard_map/ppermute | solution.py:259
  6.6 12.1 %collective-permute-start = (bf16[96,640]{1,0:T(8,128)(2,1)S(1)}, bf16[96,640]{1,0:T(8,128)(2,1)S(1)}, u32[]{:S(2)}, u32[]{:S(2)}) collective-permute-start(bf16[96,640]{1,0:T(8,128)(2,1)S(1)} %get-tuple-element.17), channel_id=1, source_target_pairs={{0,2},{2,0},{4,6},{6,4},{8,10},{10,8},{12,14},{14,12},{1,3},{3,1},... | collective-permute-start | bytes 368648 | tf_op jit(solution)/shard_map/ppermute | solution.py:259
  7.2 11.5 %collective-permute-start.6 = (bf16[96,640]{1,0:T(8,128)(2,1)S(1)}, bf16[96,640]{1,0:T(8,128)(2,1)S(1)}, u32[]{:S(2)}, u32[]{:S(2)}) collective-permute-start(bf16[96,640]{1,0:T(8,128)(2,1)S(1)} %shard_map.38.refs_7_), channel_id=1, source_target_pairs={{0,4},{2,6},{4,0},{6,2},{8,12},{10,14},{12,8},{14,10},{1,5},{3,7},... | collective-permute-start | bytes 368648 | tf_op jit(solution)/shard_map/ppermute | solution.py:259
  8.9 6.9 %collective-permute-start.4 = (bf16[48,640]{1,0:T(8,128)(2,1)S(1)}, bf16[48,640]{1,0:T(8,128)(2,1)S(1)}, u32[]{:S(2)}, u32[]{:S(2)}) collective-permute-start(bf16[48,640]{1,0:T(8,128)(2,1)S(1)} %get-tuple-element.21), channel_id=1, source_target_pairs={{0,10},{2,8},{4,14},{6,12},{8,2},{10,0},{12,6},{14,4},{1,11},{3,9}... | collective-permute-start | bytes 184328 | tf_op jit(solution)/shard_map/ppermute | solution.py:259
  13.1 5.7 %collective-permute-start.3 = (bf16[48,640]{1,0:T(8,128)(2,1)S(1)}, bf16[48,640]{1,0:T(8,128)(2,1)S(1)}, u32[]{:S(2)}, u32[]{:S(2)}) collective-permute-start(bf16[48,640]{1,0:T(8,128)(2,1)S(1)} %get-tuple-element.20.refs_4_), channel_id=1, source_target_pairs={{0,8},{2,10},{4,12},{6,14},{8,0},{10,2},{12,4},{14,6},{1,9},{3,11}... | collective-permute-start | bytes 184328 | tf_op jit(solution)/shard_map/ppermute | solution.py:259
  13.1 5.6 %collective-permute-start.2 = (bf16[48,640]{1,0:T(8,128)(2,1)S(1)}, bf16[48,640]{1,0:T(8,128)(2,1)S(1)}, u32[]{:S(2)}, u32[]{:S(2)}) collective-permute-start(bf16[48,640]{1,0:T(8,128)(2,1)S(1)} %get-tuple-element.19), channel_id=1, source_target_pairs={{0,2},{2,0},{4,6},{6,4},{8,10},{10,8},{12,14},{14,12},{1,3},{3,1},... | collective-permute-start | bytes 184328 | tf_op jit(solution)/shard_map/ppermute | solution.py:259
  19.3 4.4 %collective-permute-start.7 = (bf16[48,768]{1,0:T(8,128)(2,1)S(1)}, bf16[48,768]{1,0:T(8,128)(2,1)S(1)}, u32[]{:S(2)}, u32[]{:S(2)}) collective-permute-start(bf16[48,768]{1,0:T(8,128)(2,1)S(1)} %get-tuple-element.23), channel_id=1, source_target_pairs={{0,2},{2,0},{4,6},{6,4},{8,10},{10,8},{12,14},{14,12},{1,3},{3,1},... | collective-permute-start | bytes 221192 | tf_op jit(solution)/shard_map/ppermute | solution.py:259
  19.4 5.3 %collective-permute-start.8 = (bf16[48,768]{1,0:T(8,128)(2,1)S(1)}, bf16[48,768]{1,0:T(8,128)(2,1)S(1)}, u32[]{:S(2)}, u32[]{:S(2)}) collective-permute-start(bf16[48,768]{1,0:T(8,128)(2,1)S(1)} %get-tuple-element.24), channel_id=1, source_target_pairs={{0,6},{2,4},{4,2},{6,0},{8,14},{10,12},{12,10},{14,8},{1,7},{3,5},... | collective-permute-start | bytes 221192 | tf_op jit(solution)/shard_map/ppermute | solution.py:259
  20.8 5.2 %collective-permute-start.9 = (bf16[48,768]{1,0:T(8,128)(2,1)S(1)}, bf16[48,768]{1,0:T(8,128)(2,1)S(1)}, u32[]{:S(2)}, u32[]{:S(2)}) collective-permute-start(bf16[48,768]{1,0:T(8,128)(2,1)S(1)} %get-tuple-element.26), channel_id=1, source_target_pairs={{0,4},{2,6},{4,0},{6,2},{8,12},{10,14},{12,8},{14,10},{1,5},{3,7},... | collective-permute-start | bytes 221192 | tf_op jit(solution)/shard_map/ppermute | solution.py:259
